TPU v7x, 32 devices: a whole 2x2x4 slice. The times are simulated.
32 devices in a mesh: dp: 16 (over z, y, x), rep: 2 (over core).
Axes of the slice: x: 2, y: 2, z: 4, core: 2. Of those that a mesh axis runs over, the one named last changes fastest.
Arguments:
- tokens: bfloat16 [65536, 768], P(('dp', 'rep')), may hold values from -6 to 6
- flags: int32 [65536], P(('dp', 'rep')), may hold values from 0 to 1, as said below
- mask_embed: bfloat16 [768], replicated, may hold values from -6 to 6
- cotangent: bfloat16 [65536, 768], P(('dp', 'rep')), may hold values from -6 to 6
- w_qkv: float32 [768, 2304], P('dp'), may hold values from -0.21875 to 0.21875
- b_qv: float32 [2, 768], P(None, 'dp'), may hold values from -4 to 4
- w_out: float32 [768, 768], P('dp'), may hold values from -1.25 to 1.25
- b_out: float32 [768], P('dp'), may hold values from -4 to 4
- norm_one: float32 [2, 768], P(None, 'dp'), as said below
- w_up: float32 [768, 3072], P('dp'), may hold values from -0.21875 to 0.21875
- b_up: float32 [3072], P('dp'), may hold values from -4 to 4
- w_down: float32 [3072, 768], P('dp'), may hold values from -0.109375 to 0.109375
- b_down: float32 [768], P('dp'), may hold values from -4 to 4
- norm_two: float32 [2, 768], P(None, 'dp'), as said below
Outputs:
- activations: bfloat16 [65536, 768], P(('dp', 'rep'))
- input_grad: float32 [65536, 768], P(('dp', 'rep'))
- grad_w_qkv: float32 [768, 2304], P('dp')
- grad_b_qv: float32 [2, 768], P(None, 'dp')
- grad_w_out: float32 [768, 768], P('dp')
- grad_b_out: float32 [768], P('dp')
- grad_norm_one: float32 [2, 768], P(None, 'dp')
- grad_w_up: float32 [768, 3072], P('dp')
- grad_b_up: float32 [3072], P('dp')
- grad_w_down: float32 [3072, 768], P('dp')
- grad_b_down: float32 [768], P('dp')
- grad_norm_two: float32 [2, 768], P(None, 'dp')
Inputs may be any that keep to these rules, and one draw needn't show every extreme that they name: `flags`: within each sequence of 512 tokens the ones form spans; the share of masked tokens differs from sequence to sequence. `norm_one`: row 0 is a gain near 1, row 1 a shift. `norm_two`: row 0 is a gain near 1, row 1 a shift.
All inputs are finite; a program needn't handle non-finite values.
Results may differ from a plain program's by a relative error of at most 0.015.
Values may be sent and summed in bfloat16 or wider, within the bound.
A program may use at most 320 MiB of HBM per device.

v0:
```python
import jax
import jax.numpy as jnp
from jax import lax
from jax.sharding import PartitionSpec as P

HEADS = 12
SEQ = 512


epsilon = 1e-12


def normalize(values, gain, shift):
    center = values - jnp.mean(values, axis=-1, keepdims=True)
    inverse = lax.rsqrt(jnp.mean(center * center, axis=-1, keepdims=True) + epsilon)
    unit = center * inverse
    return (unit * gain + shift, unit, inverse)


def normalize_back(grad_out, unit, inverse, gain):
    scaled = grad_out * gain
    return inverse * (
        scaled
        - jnp.mean(scaled, axis=-1, keepdims=True)
        - unit * jnp.mean(scaled * unit, axis=-1, keepdims=True)
    )


def gelu_slope(values):
    return (
        0.5 * (1.0 + lax.erf(values * 0.7071067811865476))
        + values * jnp.exp(-0.5 * values * values) * 0.3989422804014327
    )


def local(
    tokens,
    flags,
    mask_embed,
    cotangent,
    w_qkv,
    b_qv,
    w_out,
    b_out,
    norm_one,
    w_up,
    b_up,
    w_down,
    b_down,
    norm_two,
):
    half = jnp.bfloat16
    single = jnp.float32
    full = (
        lax.all_gather(w_qkv.astype(half), "dp", axis=0, tiled=True),
        lax.all_gather(w_out.astype(half), "dp", axis=0, tiled=True),
        lax.all_gather(w_up.astype(half), "dp", axis=0, tiled=True),
        lax.all_gather(w_down.astype(half), "dp", axis=0, tiled=True),
        lax.all_gather(b_qv.astype(half), "dp", axis=1, tiled=True),
        lax.all_gather(b_out.astype(half), "dp", axis=0, tiled=True),
        lax.all_gather(norm_one.astype(half), "dp", axis=1, tiled=True),
        lax.all_gather(b_up.astype(half), "dp", axis=0, tiled=True),
        lax.all_gather(b_down.astype(half), "dp", axis=0, tiled=True),
        lax.all_gather(norm_two.astype(half), "dp", axis=1, tiled=True),
    )
    (
        qkv_full,
        out_full,
        up_full,
        down_full,
        bqv_full,
        bout_full,
        first_norm,
        bup_full,
        bdown_full,
        second_norm,
    ) = full
    width = qkv_full.shape[0]
    head_size = width // HEADS
    count = tokens.shape[0]
    groups = count // SEQ
    scale = head_size ** (-0.5)
    masked = (flags > 0)[:, None]
    inputs = jnp.where(masked, mask_embed[None, :], tokens)
    bias_qv = bqv_full.astype(single)
    qkv_bias = jnp.concatenate([bias_qv[0], jnp.zeros_like(bias_qv[0]), bias_qv[1]])
    projected = (jnp.dot(inputs, qkv_full, preferred_element_type=single) + qkv_bias).astype(half)
    query = projected[:, :width].reshape(groups, SEQ, HEADS, head_size)
    keys = projected[:, width : 2 * width].reshape(groups, SEQ, HEADS, head_size)
    vals = projected[:, 2 * width :].reshape(groups, SEQ, HEADS, head_size)
    scores = jnp.einsum("bqhe,bkhe->bhqk", query, keys, preferred_element_type=single) * scale
    row_max = jnp.max(scores, axis=-1, keepdims=True)
    expo = jnp.exp(scores - row_max)
    total = jnp.sum(expo, axis=-1, keepdims=True)
    log_total = row_max + jnp.log(total)
    weights = (expo / total).astype(half)
    mixed = (
        jnp.einsum("bhqk,bkhe->bqhe", weights, vals, preferred_element_type=single)
        .reshape(count, width)
        .astype(half)
    )
    attended = jnp.dot(mixed, out_full, preferred_element_type=single) + bout_full.astype(single)
    gain_one = first_norm.astype(single)
    first, unit_one, inverse_one = normalize(
        inputs.astype(single) + attended, gain_one[0], gain_one[1]
    )
    first_low = first.astype(half)
    upper = jnp.dot(first_low, up_full, preferred_element_type=single) + bup_full.astype(single)
    acts = jax.nn.gelu(upper, approximate=False).astype(half)
    lowered = jnp.dot(acts, down_full, preferred_element_type=single) + bdown_full.astype(single)
    gain_two = second_norm.astype(single)
    second, unit_two, inverse_two = normalize(first + lowered, gain_two[0], gain_two[1])
    activations = second.astype(half)
    qkv_back, out_back, up_back, down_back, norm_one_back, norm_two_back = (
        lax.all_gather(w_qkv.astype(half), "dp", axis=0, tiled=True),
        lax.all_gather(w_out.astype(half), "dp", axis=0, tiled=True),
        lax.all_gather(w_up.astype(half), "dp", axis=0, tiled=True),
        lax.all_gather(w_down.astype(half), "dp", axis=0, tiled=True),
        lax.all_gather(norm_one.astype(half), "dp", axis=1, tiled=True),
        lax.all_gather(norm_two.astype(half), "dp", axis=1, tiled=True),
    )
    gain_one_back = norm_one_back.astype(single)
    gain_two_back = norm_two_back.astype(single)
    out_grad = jnp.where(masked, cotangent.astype(single), single(0.0))
    grad_norm_two = jnp.stack([jnp.sum(out_grad * unit_two, axis=0), jnp.sum(out_grad, axis=0)])
    d_second = normalize_back(out_grad, unit_two, inverse_two, gain_two_back[0])
    d_lowered = d_second.astype(half)
    grad_w_down = jnp.einsum("tf,td->fd", acts, d_lowered, preferred_element_type=single)
    grad_b_down = jnp.sum(d_lowered.astype(single), axis=0)
    d_acts = jnp.einsum("td,fd->tf", d_lowered, down_back, preferred_element_type=single)
    d_upper = (d_acts * gelu_slope(upper)).astype(half)
    grad_w_up = jnp.einsum("td,tf->df", first_low, d_upper, preferred_element_type=single)
    grad_b_up = jnp.sum(d_upper.astype(single), axis=0)
    d_first = d_second + jnp.einsum("tf,df->td", d_upper, up_back, preferred_element_type=single)
    grad_norm_one = jnp.stack([jnp.sum(d_first * unit_one, axis=0), jnp.sum(d_first, axis=0)])
    d_sum = normalize_back(d_first, unit_one, inverse_one, gain_one_back[0])
    d_attended = d_sum.astype(half)
    grad_w_out = jnp.einsum("tc,td->cd", mixed, d_attended, preferred_element_type=single)
    grad_b_out = jnp.sum(d_attended.astype(single), axis=0)
    d_mixed = jnp.einsum("td,cd->tc", d_attended, out_back, preferred_element_type=single).astype(
        half
    )
    d_mixed = d_mixed.reshape(groups, SEQ, HEADS, head_size)
    again_scores = jnp.einsum("bqhe,bkhe->bhqk", query, keys, preferred_element_type=single) * scale
    probs = jnp.exp(again_scores - log_total)
    probs_low = probs.astype(half)
    d_probs = jnp.einsum("bqhe,bkhe->bhqk", d_mixed, vals, preferred_element_type=single)
    d_vals = jnp.einsum("bhqk,bqhe->bkhe", probs_low, d_mixed, preferred_element_type=single)
    d_scores = (probs * (d_probs - jnp.sum(d_probs * probs, axis=-1, keepdims=True))).astype(half)
    d_query = jnp.einsum("bhqk,bkhe->bqhe", d_scores, keys, preferred_element_type=single) * scale
    d_keys = jnp.einsum("bhqk,bqhe->bkhe", d_scores, query, preferred_element_type=single) * scale
    d_projected = jnp.concatenate(
        [d_query.reshape(count, width), d_keys.reshape(count, width), d_vals.reshape(count, width)],
        axis=1,
    ).astype(half)
    grad_w_qkv = jnp.einsum("td,tf->df", inputs, d_projected, preferred_element_type=single)
    column_sums = jnp.sum(d_projected.astype(single), axis=0)
    grad_b_qv = jnp.stack([column_sums[:width], column_sums[2 * width :]])
    d_inputs = jnp.einsum("tf,df->td", d_projected, qkv_back, preferred_element_type=single) + d_sum
    input_grad = jnp.where(masked, single(0.0), d_inputs)
    shards = (
        lax.psum_scatter(grad_w_qkv, "dp", scatter_dimension=0, tiled=True),
        lax.psum_scatter(grad_w_out, "dp", scatter_dimension=0, tiled=True),
        lax.psum_scatter(grad_w_up, "dp", scatter_dimension=0, tiled=True),
        lax.psum_scatter(grad_w_down, "dp", scatter_dimension=0, tiled=True),
        lax.psum_scatter(grad_b_qv, "dp", scatter_dimension=1, tiled=True),
        lax.psum_scatter(grad_b_out, "dp", scatter_dimension=0, tiled=True),
        lax.psum_scatter(grad_norm_one, "dp", scatter_dimension=1, tiled=True),
        lax.psum_scatter(grad_b_up, "dp", scatter_dimension=0, tiled=True),
        lax.psum_scatter(grad_b_down, "dp", scatter_dimension=0, tiled=True),
        lax.psum_scatter(grad_norm_two, "dp", scatter_dimension=1, tiled=True),
    )
    summed = (
        lax.psum(shards[0].astype(jnp.bfloat16), "rep").astype(jnp.float32),
        lax.psum(shards[1].astype(jnp.bfloat16), "rep").astype(jnp.float32),
        lax.psum(shards[2].astype(jnp.bfloat16), "rep").astype(jnp.float32),
        lax.psum(shards[3].astype(jnp.bfloat16), "rep").astype(jnp.float32),
        lax.psum(shards[4].astype(jnp.bfloat16), "rep").astype(jnp.float32),
        lax.psum(shards[5].astype(jnp.bfloat16), "rep").astype(jnp.float32),
        lax.psum(shards[6].astype(jnp.bfloat16), "rep").astype(jnp.float32),
        lax.psum(shards[7].astype(jnp.bfloat16), "rep").astype(jnp.float32),
        lax.psum(shards[8].astype(jnp.bfloat16), "rep").astype(jnp.float32),
        lax.psum(shards[9].astype(jnp.bfloat16), "rep").astype(jnp.float32),
    )
    (
        sum_qkv,
        sum_out,
        sum_up,
        sum_down,
        sum_bqv,
        sum_bout,
        sum_norm_one,
        sum_bup,
        sum_bdown,
        sum_norm_two,
    ) = summed
    return (
        activations,
        input_grad,
        sum_qkv,
        sum_bqv,
        sum_out,
        sum_bout,
        sum_norm_one,
        sum_up,
        sum_bup,
        sum_down,
        sum_bdown,
        sum_norm_two,
    )


def solution(mesh):
    return jax.shard_map(
        local,
        mesh=mesh,
        in_specs=(
            P(("dp", "rep"), None),
            P(("dp", "rep")),
            P(),
            P(("dp", "rep"), None),
            P("dp", None),
            P(None, "dp"),
            P("dp", None),
            P("dp"),
            P(None, "dp"),
            P("dp", None),
            P("dp"),
            P("dp", None),
            P("dp"),
            P(None, "dp"),
        ),
        out_specs=(
            P(("dp", "rep"), None),
            P(("dp", "rep"), None),
            P("dp", None),
            P(None, "dp"),
            P("dp", None),
            P("dp"),
            P(None, "dp"),
            P("dp", None),
            P("dp"),
            P("dp", None),
            P("dp"),
            P(None, "dp"),
        ),
        check_vma=False,
    )
```

profile of v0, /device:TPU:0, one launch (start us, length us, event | category | flops | bytes accessed | tf_op | source)
XLA Modules:
  0.0 1622.7 jit_solution(15811087074789924663)
XLA Ops:
  22.6 80.0 %all-reduce.7 = (bf16[768]{0:T(1024)(128)(2,1)S(1)}, bf16[3072]{0:T(1024)(128)(2,1)S(1)}, bf16[768]{0:T(1024)(128)(2,1)S(1)}) all-reduce(bf16[768]{0:T(1024)(128)(2,1)S(1)} %dynamic-update-slice, bf16[3072]{0:T(1024)(128)(2,1)S(1)} %dynamic-update-slice.1, bf16[768]{0:T(1024)(128)(2,1)S(1)} %dynamic-update-slice.2), channel_id=1, replica_groups=mesh['dp'=16,'rep'=2] {'dp'}, use_global_device_ids=true, to_apply=%add | all-reduce | flops 4608 | bytes 18432
  103.2 35.5 %all-gather.2 = bf16[16,48,2]{1,2,0:T(2,128)(2,1)S(1)} all-gather(bf16[1,48,2]{1,2,0:T(2,128)(2,1)S(1)} %convert_bitcast_fusion.2), channel_id=1, replica_groups=mesh['dp'=16,'rep'=2] {'dp'}, dimensions={0}, use_global_device_ids=true | all-gather | bytes 3264 | tf_op jit(solution)/shard_map/all_gather | solution.py:64
  138.7 37.6 %all-gather.1 = bf16[16,48,2]{1,2,0:T(2,128)(2,1)S(1)} all-gather(bf16[1,48,2]{1,2,0:T(2,128)(2,1)S(1)} %convert_bitcast_fusion.3), channel_id=1, replica_groups=mesh['dp'=16,'rep'=2] {'dp'}, dimensions={0}, use_global_device_ids=true | all-gather | bytes 3264 | tf_op jit(solution)/shard_map/all_gather | solution.py:61
  176.3 36.5 %all-gather = bf16[16,48,2]{1,2,0:T(2,128)(2,1)S(1)} all-gather(bf16[1,48,2]{1,2,0:T(2,128)(2,1)S(1)} %convert_bitcast_fusion.4), channel_id=1, replica_groups=mesh['dp'=16,'rep'=2] {'dp'}, dimensions={0}, use_global_device_ids=true | all-gather | bytes 3264 | tf_op jit(solution)/shard_map/all_gather | solution.py:59
  264.7 21.3 %multiply_reduce_fusion.1 = (f32[4,12,512]{2,1,0:T(8,128)S(1)}, f32[4,12,512,512]{2,3,1,0:T(8,128)}) fusion(bf16[4,512,12,64]{1,0,3,2:T(4,128)(2,1)} %reshape.109, bf16[4,512,12,64]{1,0,3,2:T(4,128)(2,1)S(1)} %reshape.108), kind=kOutput, calls=%fused_computation.6 | convolution fusion | flops 1635753984 | bytes 56721408 | tf_op jit(solution)/shard_map/bqhe,bkhe->bhqk/dot_general | solution.py:91
  286.0 20.1 %fusion = f32[4,12,512]{2,1,0:T(8,128)S(1)} fusion(f32[4,12,512,512]{2,3,1,0:T(8,128)} %get-tuple-element.103, f32[4,12,512]{2,1,0:T(8,128)S(1)} %get-tuple-element.102), kind=kLoop, calls=%fused_computation.5 | loop fusion | flops 37724160 | bytes 50528256 | tf_op jit(solution)/shard_map/reduce_sum | solution.py:94
  306.7 19.4 %convert_bitcast_fusion.1 = bf16[4,512,12,64]{1,3,2,0:T(8,128)(2,1)S(1)} fusion(f32[4,12,512,512]{2,3,1,0:T(8,128)} %get-tuple-element.103, f32[4,12,512]{2,1,0:T(8,128)S(1)} %fusion, f32[4,12,512]{2,1,0:T(8,128)S(1)} %get-tuple-element.102, bf16[4,512,12,64]{1,0,3,2:T(4,128)(2,1)S(1)} %copy-done.7), kind=kOutput, calls=%fused_computation.71 | convolution fusion | flops 1662517248 | bytes 56819712 | tf_op jit(solution)/shard_map/bhqk,bkhe->bqhe/dot_general | solution.py:98
  340.8 64.7 %fusion.6 = (bf16[2048,3072]{1,0:T(8,128)(2,1)}, f32[2048,3072]{1,0:T(8,128)}) fusion(f32[3072]{0:T(1024)S(1)} %convert_element_type.194, bf16[768,3072]{1,0:T(8,128)(2,1)} %all-gather.12.cloned.1.call-done, bf16[2048,768]{0,1:T(8,128)(2,1)S(1)} %fusion.63.clone.4), kind=kOutput, calls=%fused_computation.13 | convolution fusion | flops 10078912512 | bytes 45625344 | tf_op jit(solution)/shard_map/dot_general | solution.py:108
  405.6 18.0 %fusion.69 = (f32[2048]{0:T(1024)S(1)}, f32[2048,768]{0,1:T(8,128)}) fusion(f32[768]{0:T(1024)S(1)} %copy-done.44, bf16[2048,3072]{1,0:T(8,128)(2,1)} %get-tuple-element.106, bf16[3072,768]{1,0:T(8,128)(2,1)} %all-gather.14.cloned.1.call-done, f32[768]{0:T(1024)S(1)} %copy-done.35, f32[768]{0:T(1024)S(1)} %copy-done.28, f32[2048]{0:T(1024)S(1)} %copy-done.25, ...), kind=kOutput, calls=%fused_computation.132 | convolution fusion | flops 9674684416 | bytes 29918208 | tf_op jit(solution)/shard_map/dot_general | solution.py:110
  437.9 26.6 %convert_reduce_fusion = (f32[3072]{0:T(1024)}, bf16[2048,3072]{1,0:T(8,128)(2,1)}) fusion(f32[2048,3072]{1,0:T(8,128)} %get-tuple-element.107, f32[3072]{0:T(1024)S(1)} %convert_element_type.194, bf16[2048,768]{0,1:T(8,128)(2,1)S(1)} %get-tuple-element.91, bf16[3072,768]{1,0:T(8,128)(2,1)S(1)} %bitcast.107), kind=kOutput, calls=%fused_computation.20 | convolution fusion | flops 9745462272 | bytes 45637632 | tf_op jit(solution)/shard_map/td,fd->tf/dot_general | solution.py:130
  464.5 20.7 %multiply_reduce_fusion.3 = (f32[768]{0:T(1024)}, f32[2048]{0:T(1024)S(1)}, f32[2048]{0:T(1024)S(1)}, f32[768]{0:T(1024)}, f32[2048,768]{0,1:T(8,128)}) fusion(f32[2048,768]{0,1:T(8,128)} %copy-done.1, f32[2048]{0:T(1024)S(1)} %copy-done.25, f32[2048]{0:T(1024)S(1)} %copy-done.22, f32[768]{0:T(1024)S(1)} %copy-done.28, ...), kind=kOutput, calls=%fused_computation.43 | convolution fusion | flops 9693554688 | bytes 39401472 | tf_op jit(solution)/shard_map/tf,df->td/dot_general | solution.py:134
  512.3 20.2 %convert_bitcast_fusion = bf16[4,512,12,64]{1,3,2,0:T(8,128)(2,1)} fusion(f32[4,12,512,512]{2,3,1,0:T(8,128)} %get-tuple-element.103, f32[4,12,512]{2,1,0:T(8,128)S(1)} %copy-done.20, bf16[4,512,12,64]{1,0,3,2:T(4,128)(2,1)S(1)} %reshape.110), kind=kOutput, calls=%fused_computation.70 | convolution fusion | flops 1649934336 | bytes 56721408 | tf_op jit(solution)/shard_map/bhqk,bqhe->bkhe/dot_general | solution.py:148
  532.5 35.4 %multiply_reduce_fusion = (f32[4,12,512]{2,1,0:T(8,128)S(1)}, f32[4,12,512,512]{2,3,1,0:T(8,128)}) fusion(f32[4,12,512,512]{2,3,1,0:T(8,128)} %get-tuple-element.103, f32[4,12,512]{2,1,0:T(8,128)S(1)} %copy-done.20, bf16[4,512,12,64]{1,0,3,2:T(4,128)(2,1)} %reshape.107, bf16[4,512,12,64]{1,0,3,2:T(4,128)(2,1)S(1)} %reshape.110), kind=kOutput, calls=%fused_computation.1 | convolution fusion | flops 1660919808 | bytes 107151360 | tf_op jit(solution)/shard_map/bqhe,bkhe->bhqk/dot_general | solution.py:147
  568.0 41.3 %multiply_convert_fusion = bf16[4,12,512,512]{2,3,1,0:T(8,128)(2,1)} fusion(f32[4,12,512,512]{2,3,1,0:T(8,128)} %get-tuple-element.112, f32[4,12,512,512]{2,3,1,0:T(8,128)} %get-tuple-element.103, f32[4,12,512]{2,1,0:T(8,128)S(1)} %get-tuple-element.111, f32[4,12,512]{2,1,0:T(8,128)S(1)} %copy-done.20), kind=kLoop, calls=%fused_computation | loop fusion | flops 62914560 | bytes 126025728 | tf_op jit(solution)/shard_map/convert_element_type | solution.py:149
  670.7 15.4 fusion.70
  686.9 17.2 %fusion.60 = f32[768,3072]{1,0:T(8,128)} fusion(bf16[2048,3072]{1,0:T(8,128)(2,1)} %get-tuple-element.114, f32[2048,768]{0,1:T(8,128)} %copy-done.1, f32[768]{0:T(1024)S(1)} %copy-done.36, f32[768]{0:T(1024)S(1)} %copy-done.29, f32[2048]{0:T(1024)S(1)} %copy-done.26, f32[2048]{0:T(1024)S(1)} %copy-done.23), kind=kOutput, calls=%fused_computation.126 | convolution fusion | flops 9671540736 | bytes 28334080 | tf_op jit(solution)/shard_map/td,tf->df/dot_general | solution.py:132
  716.1 135.9 %reduce-scatter.14.cloned.1.call-done = f32[48,2304]{1,0:T(8,128)} async-done(((f32[768,2304]{1,0:T(8,128)}), f32[48,2304]{1,0:T(8,128)}) %reduce-scatter.14.cloned.1.call-update) | async-done | bytes 442384 | tf_op jit(solution)/shard_map/reduce_scatter | solution.py:162
  853.7 175.0 %reduce-scatter.20.cloned.1.call-done = f32[192,768]{1,0:T(8,128)} async-done(((f32[3072,768]{1,0:T(8,128)}), f32[192,768]{1,0:T(8,128)}) %reduce-scatter.20.cloned.1.call-update) | async-done | bytes 589840 | tf_op jit(solution)/shard_map/reduce_scatter | solution.py:165
  1030.6 174.3 %reduce-scatter.18.cloned.1.call-done = f32[48,3072]{1,0:T(8,128)} async-done(((f32[768,3072]{1,0:T(8,128)}), f32[48,3072]{1,0:T(8,128)}) %reduce-scatter.18.cloned.1.call-update) | async-done | bytes 589840 | tf_op jit(solution)/shard_map/reduce_scatter | solution.py:164
  1220.9 75.1 %all-reduce.6 = (bf16[768]{0:T(1024)(128)(2,1)S(1)}, bf16[3072]{0:T(1024)(128)(2,1)S(1)}, bf16[768]{0:T(1024)(128)(2,1)S(1)}) all-reduce(f32[768]{0:T(1024)S(1)} %copy-done.37, f32[3072]{0:T(1024)S(1)} %copy-done.41, f32[768]{0:T(1024)S(1)} %copy-done.33), channel_id=5, replica_groups=mesh['dp'=16,'rep'=2] {'dp'}, use_global_device_ids=true, to_apply=%region_19.20.clone | all-reduce | flops 4608 | bytes 27648
  1305.6 26.9 %reduce-scatter.26.cloned.1.call-done = f32[48,2]{1,0:T(8,128)} async-done(((f32[768,2]{1,0:T(8,128)}), f32[48,2]{1,0:T(8,128)}) %reduce-scatter.26.cloned.1.call-update) | async-done | bytes 400
  1333.3 126.4 %reduce-scatter.24.cloned.1.call-done = f32[48,2]{1,0:T(8,128)} async-done(((f32[768,2]{1,0:T(8,128)}), f32[48,2]{1,0:T(8,128)}) %reduce-scatter.24.cloned.1.call-update) | async-done | bytes 400
  1460.5 126.5 %reduce-scatter.22.cloned.1.call-done = f32[48,2]{1,0:T(8,128)} async-done(((f32[768,2]{1,0:T(8,128)}), f32[48,2]{1,0:T(8,128)}) %reduce-scatter.22.cloned.1.call-update) | async-done | bytes 400
  1593.6 14.9 all-reduce.12.cloned.1.call-done
  (241 shorter events, 239.7 us)
Async XLA Ops:
  7.2 211.4 %copy-start.14 = (bf16[2048,768]{1,0:T(8,128)(2,1)S(1)}, bf16[2048,768]{1,0:T(8,128)(2,1)}, u32[]{:S(2)}) copy-start(bf16[2048,768]{1,0:T(8,128)(2,1)} %param.17) | copy-start | bytes 9437188
  7.2 214.2 %all-gather.8.cloned.1.call-start = ((), (), s32[]{:S(2)}) async-start(), calls=%async_computation.7 | async-start | bytes 3760128 | tf_op jit(solution)/shard_map/all_gather | solution.py:55
  9.1 322.1 %all-gather.10.cloned.1.call-start = ((), (), s32[]{:S(2)}) async-start(), calls=%async_computation.8 | async-start | bytes 1253376 | tf_op jit(solution)/shard_map/all_gather | solution.py:56
  10.7 330.0 %all-gather.12.cloned.1.call-start = ((), (), s32[]{:S(2)}) async-start(), calls=%async_computation.9 | async-start | bytes 5013504 | tf_op jit(solution)/shard_map/all_gather | solution.py:57
  12.6 392.9 %all-gather.14.cloned.1.call-start = ((), (), s32[]{:S(2)}) async-start(), calls=%async_computation.10 | async-start | bytes 5013504 | tf_op jit(solution)/shard_map/all_gather | solution.py:58
  14.5 700.0 %reduce-scatter.16.cloned.1.call-start = ((), (), s32[]{:S(2)}) async-start(), calls=%async_computation.12 | async-start | bytes 2506752 | tf_op jit(solution)/shard_map/reduce_scatter | solution.py:163
  21.9 309.3 %copy-start.31 = (pred[2048]{0:T(1024)(128)(4,1)}, pred[2048]{0:T(1024)(128)(4,1)S(1)}, u32[]{:S(2)}) copy-start(pred[2048]{0:T(1024)(128)(4,1)S(1)} %broadcast_compare_fusion) | copy-start | bytes 6148
  213.0 124.7 %copy-start.27 = (f32[768]{0:T(1024)}, f32[768]{0:T(1024)S(1)}, u32[]{:S(2)}) copy-start(f32[768]{0:T(1024)S(1)} %get-tuple-element.70) | copy-start | bytes 9220
  213.0 124.7 %copy-start.34 = (f32[768]{0:T(1024)}, f32[768]{0:T(1024)S(1)}, u32[]{:S(2)}) copy-start(f32[768]{0:T(1024)S(1)} %get-tuple-element.71) | copy-start | bytes 9220
  340.7 64.8 %copy-start.22 = (f32[2048]{0:T(1024)S(1)}, f32[2048]{0:T(1024)}, u32[]{:S(2)}) copy-start(f32[2048]{0:T(1024)} %copy-done.21) | copy-start | bytes 24580
  340.7 64.8 %copy-start.25 = (f32[2048]{0:T(1024)S(1)}, f32[2048]{0:T(1024)}, u32[]{:S(2)}) copy-start(f32[2048]{0:T(1024)} %copy-done.24) | copy-start | bytes 24580
  340.7 64.8 %copy-start.28 = (f32[768]{0:T(1024)S(1)}, f32[768]{0:T(1024)}, u32[]{:S(2)}) copy-start(f32[768]{0:T(1024)} %copy-done.27) | copy-start | bytes 9220
  340.8 64.8 %copy-start.35 = (f32[768]{0:T(1024)S(1)}, f32[768]{0:T(1024)}, u32[]{:S(2)}) copy-start(f32[768]{0:T(1024)} %copy-done.34) | copy-start | bytes 9220
  340.8 64.8 %copy-start.44 = (f32[768]{0:T(1024)S(1)}, f32[768]{0:T(1024)}, u32[]{:S(2)}) copy-start(f32[768]{0:T(1024)} %convert_element_type.198) | copy-start | bytes 9220
  437.9 26.6 %copy-start.18 = (bf16[2048,768]{0,1:T(8,128)(2,1)}, bf16[2048,768]{0,1:T(8,128)(2,1)S(1)}, u32[]{:S(2)}) copy-start(bf16[2048,768]{0,1:T(8,128)(2,1)S(1)} %get-tuple-element.91) | copy-start | bytes 9437188
  567.9 284.1 %reduce-scatter.14.cloned.1.call-start = ((), (), s32[]{:S(2)}) async-start(), calls=%async_computation.11 | async-start | bytes 7520256 | tf_op jit(solution)/shard_map/reduce_scatter | solution.py:162
  568.0 41.4 %copy-start.5 = (bf16[4,512,12,64]{1,0,3,2:T(4,128)(2,1)S(1)}, bf16[4,512,12,64]{1,0,3,2:T(4,128)(2,1)}, u32[]{:S(2)}) copy-start(bf16[4,512,12,64]{1,0,3,2:T(4,128)(2,1)} %reshape.109) | copy-start | bytes 9437188
  668.8 359.9 %reduce-scatter.20.cloned.1.call-start = ((), (), s32[]{:S(2)}) async-start(), calls=%async_computation.14 | async-start | bytes 10027008 | tf_op jit(solution)/shard_map/reduce_scatter | solution.py:165
  686.2 518.7 %reduce-scatter.18.cloned.1.call-start = ((), (), s32[]{:S(2)}) async-start(), calls=%async_computation.13 | async-start | bytes 10027008 | tf_op jit(solution)/shard_map/reduce_scatter | solution.py:164
  704.1 628.3 %reduce-scatter.26.cloned.1.call-start = ((), (), s32[]{:S(2)}) async-start(), calls=%async_computation.17 | async-start | bytes 417792
  711.1 748.6 %reduce-scatter.24.cloned.1.call-start = ((), (), s32[]{:S(2)}) async-start(), calls=%async_computation.16 | async-start | bytes 417792
  712.1 874.9 %reduce-scatter.22.cloned.1.call-start = ((), (), s32[]{:S(2)}) async-start(), calls=%async_computation.15 | async-start | bytes 417792
  713.2 895.3 %all-reduce.12.cloned.1.call-start = ((), (), s32[]{:S(2)}) async-start(), calls=%async_computation.18 | async-start | bytes 1769472 | tf_op jit(solution)/shard_map/psum | solution.py:174
  1206.8 89.4 %copy-start.11 = (bf16[2048,768]{0,1:T(8,128)(2,1)S(1)}, bf16[2048,768]{0,1:T(8,128)(2,1)}, u32[]{:S(2)}) copy-start(bf16[2048,768]{0,1:T(8,128)(2,1)} %get-tuple-element.97) | copy-start | bytes 9437188
  (37 other events, 236.5 us)
Sparse Core Ops, SparseCore 0:
  11.4 74.1 all-gather.7
  88.4 54.6 all-gather.9
  146.4 78.3 all-gather.11
  228.1 78.3 all-gather.13
  568.1 127.2 reduce-scatter.15
  700.6 151.3 reduce-scatter.13
  857.7 171.0 reduce-scatter.19
  1034.4 170.4 reduce-scatter.17
  1210.1 122.2 reduce-scatter.25
  1337.5 122.0 reduce-scatter.23
  1464.9 122.0 reduce-scatter.21
  1590.0 18.4 all-reduce.11
where the time goes:
time: 1630 us; the launch traced here: 1620 us
  waiting for transfers between devices  780 us (48%)
  matrix products  337 us (21%)
  blocking collectives  267 us (16%)
  other arithmetic  119 us (7%)
  local copies, waits for them, and re-layouts  101 us (6%)
  between operations  17.9 us (1%)
    unnamed x15, waiting for transfers between devices  280 us
    reduce_scatter x1, waiting for transfers between devices, local(): lax.psum_scatter(grad_w_down, 'dp', scatter_dimension=0, tiled=True)  175 us
    reduce_scatter x1, waiting for transfers between devices, local(): lax.psum_scatter(grad_w_up, 'dp', scatter_dimension=0, tiled=True)  174 us
    unnamed x2, blocking collectives  155 us
    reduce_scatter x1, waiting for transfers between devices, local(): lax.psum_scatter(grad_w_qkv, 'dp', scatter_dimension=0, tiled=True)  136 us
    dot_general x1, matrix products, local(): jnp.dot(first_low, up_full, preferred_element_type=single)  64.7 us
    unnamed x124, local copies, waits for them, and re-layouts  47.8 us
    convert_element_type x1, other arithmetic, local(): (probs * (d_probs - jnp.sum(d_probs * probs, axis=-1, keepdims=True))).as...  41.3 us
  transfers between devices with their start and end apart: 12, of which 7 were waited for; matrix products, arithmetic and copies ran while one was open for 23% of the time, Pallas kernels for 0%

commit v1 on v0

v1 whole, which is shorter than its diff:
```python
import functools

import jax
import jax.numpy as jnp
from jax import lax
from jax.experimental import pallas as pl
from jax.experimental.pallas import tpu as pltpu
from jax.sharding import PartitionSpec as P

HEADS = 12
SEQ = 512
EPS = 1e-12
half = jnp.bfloat16
single = jnp.float32
VMEM_LIMIT = 61 * 1024 * 1024


def mm(left, right):
    return jnp.dot(left, right, preferred_element_type=single)


def mm_tb(left, right):
    return lax.dot_general(left, right, (((1,), (1,)), ((), ())), preferred_element_type=single)


def mm_ta(left, right):
    return lax.dot_general(left, right, (((0,), (0,)), ((), ())), preferred_element_type=single)


def row_mean(values):
    return jnp.mean(values, axis=-1, keepdims=True)


def col_sum(values):
    return jnp.sum(values, axis=0, keepdims=True)


def project_body(tok_ref, flag_ref, mask_ref, w_ref, bias_ref, inp_ref, proj_ref):
    masked = flag_ref[...] > 0
    inputs = jnp.where(masked, mask_ref[...].astype(single), tok_ref[...].astype(single))
    low = inputs.astype(half)
    inp_ref[...] = low
    proj_ref[...] = (mm(low, w_ref[...]) + bias_ref[...]).astype(half)


def project(tokens, flags, mask_embed, w_qkv, bias):
    count, width = tokens.shape
    block = 256
    wide = w_qkv.shape[1]
    return pl.pallas_call(
        project_body,
        grid=(count // block,),
        in_specs=[
            pl.BlockSpec((block, width), lambda i: (i, 0)),
            pl.BlockSpec((block, 1), lambda i: (i, 0)),
            pl.BlockSpec((1, width), lambda i: (0, 0)),
            pl.BlockSpec((width, wide), lambda i: (0, 0), pipeline_mode=pl.Buffered(1)),
            pl.BlockSpec((1, wide), lambda i: (0, 0)),
        ],
        out_specs=[
            pl.BlockSpec((block, width), lambda i: (i, 0)),
            pl.BlockSpec((block, wide), lambda i: (i, 0)),
        ],
        out_shape=[
            jax.ShapeDtypeStruct((count, width), half),
            jax.ShapeDtypeStruct((count, wide), half),
        ],
        compiler_params=pltpu.CompilerParams(vmem_limit_bytes=VMEM_LIMIT),
        name="project",
    )(tokens, flags, mask_embed, w_qkv, bias)


def head_masks(width):
    lane = lax.broadcasted_iota(jnp.int32, (1, width), 1)
    return [(lane // 64) == h for h in range(width // 64)]


def attend_pair(query, keys, vals):
    scaled = query * half(0.125)
    turned = vals.T
    outs, logs = [], []
    for h, mask in enumerate(head_masks(128)):
        own = jnp.where(mask, keys, half(0))
        scores = mm_tb(own, scaled)
        top = jnp.max(scores, axis=0, keepdims=True)
        expo = jnp.exp(scores - top)
        total = jnp.sum(expo, axis=0, keepdims=True)
        mixed = mm(turned[64 * h : 64 * h + 64], expo.astype(half))
        outs.append(mixed * (1.0 / total))
        logs.append(top + jnp.log(total))
    return jnp.concatenate(outs, axis=0).astype(half).T, logs


def attend_body(pairs, q_ref, k_ref, v_ref, mixed_ref, log_ref):
    for p in range(pairs):
        cols = pl.ds(128 * p, 128)
        mixed, logs = attend_pair(q_ref[:, cols], k_ref[:, cols], v_ref[:, cols])
        mixed_ref[:, cols] = mixed
        for h in range(2):
            log_ref[0, 0, pl.ds(2 * p + h, 1), :] = logs[h]


def attend(projected, pairs=2):
    count = projected.shape[0]
    width = projected.shape[1] // 3
    groups = count // SEQ
    steps = width // (128 * pairs)
    spec = lambda part: pl.BlockSpec((SEQ, 128 * pairs), lambda g, p: (g, part * steps + p))
    return pl.pallas_call(
        functools.partial(attend_body, pairs),
        grid=(groups, steps),
        in_specs=[spec(0), spec(1), spec(2)],
        out_specs=[
            pl.BlockSpec((SEQ, 128 * pairs), lambda g, p: (g, p)),
            pl.BlockSpec((1, 1, 8, SEQ), lambda g, p: (g, p, 0, 0)),
        ],
        out_shape=[
            jax.ShapeDtypeStruct((count, width), half),
            jax.ShapeDtypeStruct((groups, steps, 8, SEQ), single),
        ],
        compiler_params=pltpu.CompilerParams(vmem_limit_bytes=VMEM_LIMIT),
        name="attend",
    )(projected, projected, projected)


def attend_back_pair(query, keys, vals, grad, mixed, logs):
    scaled = query * half(0.125)
    scaled_keys = keys * half(0.125)
    product = grad.astype(single) * mixed.astype(single)
    grad_turned = grad.T
    scaled_turned = scaled.T
    d_vals, d_keys, d_query = [], [], None
    for h, mask in enumerate(head_masks(128)):
        scores = mm_tb(jnp.where(mask, scaled, half(0)), keys)
        probs = jnp.exp(scores - logs[:, h : h + 1])
        d_probs = mm_tb(jnp.where(mask, grad, half(0)), vals)
        delta = jnp.sum(jnp.where(mask, product, 0.0), axis=1, keepdims=True)
        d_scores = (probs * (d_probs - delta)).astype(half)
        rows = slice(64 * h, 64 * h + 64)
        d_vals.append(mm(grad_turned[rows], probs.astype(half)))
        d_keys.append(mm(scaled_turned[rows], d_scores))
        part = mm(d_scores, jnp.where(mask, scaled_keys, half(0)))
        d_query = part if d_query is None else d_query + part
    turn = lambda parts: jnp.concatenate(parts, axis=0).astype(half).T
    return d_query.astype(half), turn(d_keys), turn(d_vals)


def attend_back_body(pairs, q_ref, k_ref, v_ref, grad_ref, mixed_ref, log_ref, dq_ref, dk_ref, dv_ref):
    logs = log_ref[0, 0].T
    for p in range(pairs):
        cols = pl.ds(128 * p, 128)
        dq, dk, dv = attend_back_pair(
            q_ref[:, cols],
            k_ref[:, cols],
            v_ref[:, cols],
            grad_ref[:, cols],
            mixed_ref[:, cols],
            logs[:, 2 * p : 2 * p + 2],
        )
        dq_ref[:, cols] = dq
        dk_ref[:, cols] = dk
        dv_ref[:, cols] = dv


def attend_back(projected, d_mixed, mixed, logs, pairs=2):
    count, width = mixed.shape
    groups = count // SEQ
    steps = width // (128 * pairs)
    spec = lambda part: pl.BlockSpec((SEQ, 128 * pairs), lambda g, p: (g, part * steps + p))
    out = pl.BlockSpec((SEQ, 128 * pairs), lambda g, p: (g, p))
    return pl.pallas_call(
        functools.partial(attend_back_body, pairs),
        grid=(groups, steps),
        in_specs=[
            spec(0),
            spec(1),
            spec(2),
            out,
            out,
            pl.BlockSpec((1, 1, 8, SEQ), lambda g, p: (g, p, 0, 0)),
        ],
        out_specs=[out] * 3,
        out_shape=[jax.ShapeDtypeStruct((count, width), half)] * 3,
        compiler_params=pltpu.CompilerParams(vmem_limit_bytes=VMEM_LIMIT),
        name="attend_back",
    )(projected, projected, projected, d_mixed, mixed, logs)


def norm(values, gain, shift):
    center = values - row_mean(values)
    inverse = lax.rsqrt(row_mean(center * center) + EPS)
    unit = center * inverse
    return unit * gain + shift, unit, inverse


def norm_back(grad, unit, inverse, gain):
    scaled = grad * gain
    return inverse * (scaled - row_mean(scaled) - unit * row_mean(scaled * unit))


def middle_body(
    mixed_ref,
    inp_ref,
    flag_ref,
    cot_ref,
    vec_ref,
    bup_ref,
    wo_ref,
    wu_ref,
    wd_ref,
    act_out,
    dsum_out,
    dmix_out,
    small_out,
    gbup_out,
    gwo_out,
    gwu_out,
    gwd_out,
    unit1,
    first,
    low,
    acts,
    slope,
    total,
    d_low,
    acc_o,
    acc_u,
    acc_d,
    stage,
    sems,
):
    step = pl.program_id(0)
    last = pl.num_programs(0) - 1
    width = wo_ref.shape[0]
    chunks = wd_ref.shape[0] // width

    @pl.when(step == 0)
    def _():
        small_out[...] = jnp.zeros_like(small_out)
        gbup_out[...] = jnp.zeros_like(gbup_out)
        acc_o[...] = jnp.zeros_like(acc_o)
        acc_u[...] = jnp.zeros_like(acc_u)
        acc_d[...] = jnp.zeros_like(acc_d)

    vec = lambda row: vec_ref[pl.ds(row, 1), :]
    attended = mm(mixed_ref[...], wo_ref[...]) + vec(2)
    value, unit, inv1 = norm(inp_ref[...].astype(single) + attended, vec(3), vec(4))
    unit1[...] = unit
    first[...] = value
    low[...] = value.astype(half)
    total[...] = jnp.zeros_like(total)

    @pl.loop(0, chunks)
    def _(j):
        cols = pl.ds(pl.multiple_of(j * width, width), width)
        upper = mm(low[...], wu_ref[:, cols]) + bup_ref[:, cols]
        phi = 0.5 * (1.0 + lax.erf(upper * 0.7071067811865476))
        act = (upper * phi).astype(half)
        acts[j] = act
        slope[j] = (phi + upper * jnp.exp(-0.5 * upper * upper) * 0.3989422804014327).astype(half)
        total[...] += mm(act, wd_ref[cols, :])

    value, unit, inv2 = norm(first[...] + total[...] + vec(5), vec(6), vec(7))
    act_out[...] = value.astype(half)
    out_grad = jnp.where(flag_ref[...] > 0, cot_ref[...].astype(single), 0.0)
    small_out[pl.ds(6, 1), :] += col_sum(out_grad * unit)
    small_out[pl.ds(7, 1), :] += col_sum(out_grad)
    d_second = norm_back(out_grad, unit, inv2, vec(6))
    lowered = d_second.astype(half)
    d_low[...] = lowered
    small_out[pl.ds(5, 1), :] += col_sum(lowered.astype(single))
    total[...] = d_second

    @pl.loop(0, chunks)
    def _(j):
        cols = pl.ds(pl.multiple_of(j * width, width), width)
        d_acts = mm_tb(d_low[...], wd_ref[cols, :])
        d_upper = (d_acts * slope[j].astype(single)).astype(half)
        gbup_out[:, cols] += col_sum(d_upper.astype(single))
        total[...] += mm_tb(d_upper, wu_ref[:, cols])
        acc_d[j] += mm_ta(acts[j], d_low[...])
        acc_u[j] += mm_ta(low[...], d_upper)

    d_first = total[...]
    unit = unit1[...]
    small_out[pl.ds(3, 1), :] += col_sum(d_first * unit)
    small_out[pl.ds(4, 1), :] += col_sum(d_first)
    d_sum = norm_back(d_first, unit, inv1, vec(3))
    dsum_out[...] = d_sum
    d_att = d_sum.astype(half)
    small_out[pl.ds(2, 1), :] += col_sum(d_att.astype(single))
    dmix_out[...] = mm_tb(d_att, wo_ref[...]).astype(half)
    acc_o[...] += mm_ta(mixed_ref[...], d_att)

    @pl.when(step == last)
    def _():
        copies = []
        todo = [(acc_d.at[j], gwd_out.at[pl.ds(j * width, width), :]) for j in range(chunks)]
        todo += [(acc_u.at[j], gwu_out.at[:, pl.ds(j * width, width)]) for j in range(chunks)]
        todo += [(acc_o, gwo_out)]
        for n, (src, dst) in enumerate(todo):
            slot = n % 2
            if n >= 2:
                copies[n - 2].wait()
            stage[slot] = src[...].astype(half)
            copies.append(pltpu.make_async_copy(stage.at[slot], dst, sems.at[slot]))
            copies[n].start()
        for copy in copies[-2:]:
            copy.wait()


def middle(mixed, inputs, flags, cotangent, vecs, b_up, w_out, w_up, w_down, block=512):
    count, width = mixed.shape
    hidden = w_up.shape[1]
    chunks = hidden // width
    rows = lambda cols: pl.BlockSpec((block, cols), lambda i: (i, 0))
    once = lambda shape: pl.BlockSpec(shape, lambda i: (0, 0), pipeline_mode=pl.Buffered(1))
    keep = lambda shape: pl.BlockSpec(shape, lambda i: (0, 0))
    whole = pl.BlockSpec(memory_space=pl.ANY)
    return pl.pallas_call(
        middle_body,
        grid=(count // block,),
        in_specs=[
            rows(width),
            rows(width),
            rows(1),
            rows(width),
            keep((8, width)),
            keep((1, hidden)),
            once((width, width)),
            once((width, hidden)),
            once((hidden, width)),
        ],
        out_specs=[
            rows(width),
            rows(width),
            rows(width),
            keep((8, width)),
            keep((1, hidden)),
            whole,
            whole,
            whole,
        ],
        out_shape=[
            jax.ShapeDtypeStruct((count, width), half),
            jax.ShapeDtypeStruct((count, width), single),
            jax.ShapeDtypeStruct((count, width), half),
            jax.ShapeDtypeStruct((8, width), single),
            jax.ShapeDtypeStruct((1, hidden), single),
            jax.ShapeDtypeStruct((width, width), half),
            jax.ShapeDtypeStruct((width, hidden), half),
            jax.ShapeDtypeStruct((hidden, width), half),
        ],
        scratch_shapes=[
            pltpu.VMEM((block, width), single),
            pltpu.VMEM((block, width), single),
            pltpu.VMEM((block, width), half),
            pltpu.VMEM((chunks, block, width), half),
            pltpu.VMEM((chunks, block, width), half),
            pltpu.VMEM((block, width), single),
            pltpu.VMEM((block, width), half),
            pltpu.VMEM((width, width), single),
            pltpu.VMEM((chunks, width, width), single),
            pltpu.VMEM((chunks, width, width), single),
            pltpu.VMEM((2, width, width), half),
            pltpu.SemaphoreType.DMA((2,)),
        ],
        compiler_params=pltpu.CompilerParams(vmem_limit_bytes=VMEM_LIMIT),
        name="middle",
    )(mixed, inputs, flags, cotangent, vecs, b_up, w_out, w_up, w_down)


def weight_back_body(inp_ref, dq_ref, dk_ref, dv_ref, out_ref, sum_ref):
    part = pl.program_id(0)

    def work(ref):
        grad = ref[...]
        out_ref[...] = mm_ta(inp_ref[...], grad).astype(half)
        sum_ref[...] = jnp.broadcast_to(col_sum(grad.astype(single)), sum_ref.shape)

    for n, ref in enumerate((dq_ref, dk_ref, dv_ref)):
        pl.when(part == n)(functools.partial(work, ref))


def weight_back(inputs, d_parts, block=256):
    count, width = inputs.shape
    steps = width // block

    def spec(n):
        return pl.BlockSpec(
            (count, block), lambda p, i: (0, jnp.where(p == n, i, jnp.where(p > n, steps - 1, 0)))
        )

    return pl.pallas_call(
        weight_back_body,
        grid=(3, steps),
        in_specs=[pl.BlockSpec((count, width), lambda p, i: (0, 0), pipeline_mode=pl.Buffered(1))]
        + [spec(n) for n in range(3)],
        out_specs=[
            pl.BlockSpec((width, block), lambda p, i: (0, p * steps + i)),
            pl.BlockSpec((8, block), lambda p, i: (0, p * steps + i)),
        ],
        out_shape=[
            jax.ShapeDtypeStruct((width, 3 * width), half),
            jax.ShapeDtypeStruct((8, 3 * width), single),
        ],
        compiler_params=pltpu.CompilerParams(vmem_limit_bytes=VMEM_LIMIT),
        name="weight_back",
    )(inputs, *d_parts)


def input_back_body(dq_ref, dk_ref, dv_ref, w_ref, dsum_ref, flag_ref, out_ref):
    width = dq_ref.shape[1]
    grad = dsum_ref[...]
    for part, ref in enumerate((dq_ref, dk_ref, dv_ref)):
        grad = grad + mm_tb(ref[...], w_ref[:, pl.ds(part * width, width)])
    out_ref[...] = jnp.where(flag_ref[...] > 0, 0.0, grad)


def input_back(d_parts, w_qkv, d_sum, flags, block=256):
    count, width = d_sum.shape
    spec = pl.BlockSpec((block, width), lambda i: (i, 0))
    return pl.pallas_call(
        input_back_body,
        grid=(count // block,),
        in_specs=[spec] * 3
        + [
            pl.BlockSpec(w_qkv.shape, lambda i: (0, 0), pipeline_mode=pl.Buffered(1)),
            spec,
            pl.BlockSpec((block, 1), lambda i: (i, 0)),
        ],
        out_specs=spec,
        out_shape=jax.ShapeDtypeStruct((count, width), single),
        compiler_params=pltpu.CompilerParams(vmem_limit_bytes=VMEM_LIMIT),
        name="input_back",
    )(*d_parts, w_qkv, d_sum, flags)


MESH = pl.DeviceIdType.MESH
ZS = 4


class Place:
    def __init__(self):
        self.me = lax.axis_index("dp")
        self.core = lax.axis_index("rep")
        self.z = self.me // 4
        self.y = (self.me // 2) % 2
        self.x = self.me % 2
        step_x = 1 - 2 * self.x
        step_y = 2 - 4 * self.y
        self.near = self.me + step_x + self.core * (step_y - step_x)
        self.far = self.me + step_y + self.core * (step_x - step_y)
        self.diag = self.me + step_x + step_y
        self.near_bit = self.x + self.core * (self.y - self.x)
        self.far_bit = self.y + self.core * (self.x - self.y)

    def chip(self, z, far, near):
        return z * 4 + far * (2 - self.core) + near * (1 + self.core)

    def partner(self):
        return (self.me, 1 - self.core)

    def barrier(self):
        sem = pltpu.get_barrier_semaphore()
        tell = lambda dev: pl.semaphore_signal(sem, inc=1, device_id=dev, device_id_type=MESH)
        tell(self.partner())
        tell((self.near, self.core))
        tell((self.far, self.core))

        @pl.when(self.z > 0)
        def _():
            tell((self.me - 4, self.core))

        @pl.when(self.z < ZS - 1)
        def _():
            tell((self.me + 4, self.core))

        return sem, 3 + jnp.minimum(self.z, 1) + jnp.minimum(ZS - 1 - self.z, 1)


def send(src, dst, send_sem, recv_sem, dev):
    return pltpu.make_async_remote_copy(
        src_ref=src, dst_ref=dst, send_sem=send_sem, recv_sem=recv_sem, device_id=dev, device_id_type=MESH
    )


class Gather:
    def __init__(self, place, fulls, rows, sends, recvs, passed):
        self.place = place
        self.fulls = fulls
        self.rows = rows
        self.sends, self.recvs, self.passed = sends, recvs, passed

    def piece(self, t, q, h):
        full = self.fulls[t]
        rows = self.rows[t]
        if full.shape[1] == 128:
            part = rows // 2
            return full.at[pl.ds(pl.multiple_of(q * rows + h * part, 8), part), :]
        cols = full.shape[1] // 2
        return full.at[pl.ds(pl.multiple_of(q * rows, 16), rows), pl.ds(pl.multiple_of(h * cols, 128), cols)]

    def events(self):
        p = self.place
        yes = p.z >= 0
        up = ((p.me + 4, p.core), p.z < ZS - 1)
        down = ((p.me - 4, p.core), p.z > 0)
        near = ((p.near, p.core), yes)
        far = ((p.far, p.core), yes)
        other = (p.partner(), None)
        out = [(p.me, yes, [up, down, near, far], True)]
        for r in range(ZS):
            ways = [(-4 * r, p.z >= r, up), (4 * r, p.z + r < ZS, down)] if r else [(0, yes, None)]
            if r:
                for shift, there, onward in ways:
                    out.append((p.me + shift, there, [onward, near, far, other], False))
            for shift, there, _ in ways:
                out.append((p.near + shift, there, [far, other], False))
            for shift, there, _ in ways:
                out.append((p.far + shift, there, [other], False))
            for shift, there, _ in ways:
                out.append((p.diag + shift, there, [other], False))
        return out

    def copies(self, t, event):
        q, _, targets, _ = event
        piece = self.piece(t, q, self.place.core)
        made = []
        for n, (dev, cond) in enumerate(targets):
            recv = self.passed.at[t, q] if cond is None else self.recvs.at[t, q]
            made.append((send(piece, piece, self.sends.at[t, n, q], recv, dev), cond))
        return made

    def run(self, t, event):
        q, there, targets, own = event

        @pl.when(there)
        def _():
            made = self.copies(t, event)
            if not own:
                made[0][0].wait_recv() if made[0][1] is not None else send(
                    self.piece(t, q, self.place.core),
                    self.piece(t, q, self.place.core),
                    self.sends.at[t, 0, q],
                    self.recvs.at[t, q],
                    self.place.partner(),
                ).wait_recv()
            for copy, cond in made:
                if cond is None:
                    copy.start()
                else:
                    pl.when(cond)(copy.start)

    def finish_sends(self, t, event):
        q, there, targets, own = event

        @pl.when(there)
        def _():
            for copy, cond in self.copies(t, event):
                if cond is None:
                    copy.wait_send()
                else:
                    pl.when(cond)(copy.wait_send)

    def finish_partner(self, t):
        p = self.place

        @pl.loop(0, 16)
        def _(q):
            @pl.when(q != p.me)
            def _():
                piece = self.piece(t, q, 1 - p.core)
                send(piece, piece, self.sends.at[t, 0, q], self.passed.at[t, q], p.partner()).wait_recv()


def gather_body(count, *refs):
    shards, fulls = refs[:count], refs[count : 2 * count]
    own = refs[2 * count : 3 * count]
    sends, recvs, passed, local = refs[3 * count :]
    place = Place()
    sem, expect = place.barrier()
    for shard, low in zip(shards, own):
        low[...] = shard[...].astype(low.dtype)
    rows = [shard.shape[0] for shard in shards]
    g = Gather(place, fulls, rows, sends, recvs, passed)
    mine = []
    for t in range(count):
        dst = fulls[t].at[pl.ds(pl.multiple_of(place.me * rows[t], 16), rows[t]), :]
        mine.append(pltpu.make_async_copy(own[t], dst, local.at[t]))
        mine[t].start()
    pl.semaphore_wait(sem, expect)
    events = g.events()
    for t in range(count):
        mine[t].wait()
        g.run(t, events[0])
    for event in events[1:]:
        for t in range(count):
            g.run(t, event)
    for event in events:
        for t in range(count):
            g.finish_sends(t, event)
    for t in range(count):
        g.finish_partner(t)


def gather_all(shards, dtypes, collective_id):
    count = len(shards)
    fulls = [jax.ShapeDtypeStruct((16 * s.shape[0], s.shape[1]), d) for s, d in zip(shards, dtypes)]
    return pl.pallas_call(
        functools.partial(gather_body, count),
        in_specs=[pl.BlockSpec(memory_space=pltpu.VMEM)] * count,
        out_specs=[pl.BlockSpec(memory_space=pl.ANY)] * count,
        out_shape=fulls,
        scratch_shapes=[pltpu.VMEM(s.shape, d) for s, d in zip(shards, dtypes)]
        + [
            pltpu.SemaphoreType.DMA((count, 4, 16)),
            pltpu.SemaphoreType.DMA((count, 16)),
            pltpu.SemaphoreType.DMA((count, 16)),
            pltpu.SemaphoreType.DMA((count,)),
        ],
        compiler_params=pltpu.CompilerParams(
            collective_id=collective_id, has_side_effects=True, vmem_limit_bytes=VMEM_LIMIT
        ),
        name=f"gather_{collective_id}",
    )(*shards)


class Scatter:
    def __init__(self, place, grad, rows, out, mine, pair, far, near, low, high, own, sems):
        self.place = place
        self.grad, self.rows, self.out = grad, rows, out
        self.mine, self.pair, self.far, self.near, self.low, self.high, self.own = mine, pair, far, near, low, high, own
        self.sems = sems
        self.cols = grad.shape[1] // 2

    LOCAL, PAIR_S, PAIR_R, LAST_S, LAST_R, FAR_S, FAR_R = 0, 1, 2, 3, 4, 8, 16
    NEAR_S, NEAR_R, UP_S, UP_R, DOWN_S, DOWN_R = 24, 28, 32, 36, 40, 44
    COUNT = 48

    def columns(self, h):
        return pl.ds(pl.multiple_of(h * self.cols, 128), self.cols)

    def at(self, ref, q):
        return ref.at[pl.ds(pl.multiple_of(q * self.rows, 16), self.rows), :]

    def load(self, ref, q):
        return ref[pl.ds(pl.multiple_of(q * self.rows, 16), self.rows), :].astype(single)

    def store(self, ref, q, value):
        ref[pl.ds(pl.multiple_of(q * self.rows, 16), self.rows), :] = value.astype(ref.dtype)

    def copy_local(self):
        return pltpu.make_async_copy(
            self.grad.at[:, self.columns(self.place.core)], self.mine, self.sems.at[self.LOCAL]
        )

    def copy_pair(self):
        p = self.place
        return send(
            self.grad.at[:, self.columns(1 - p.core)],
            self.pair,
            self.sems.at[self.PAIR_S],
            self.sems.at[self.PAIR_R],
            p.partner(),
        )

    def copy_far(self, k):
        p = self.place
        q = p.chip(k // 2, 1 - p.far_bit, k % 2)
        return send(
            self.at(self.mine, q),
            self.at(self.far, k),
            self.sems.at[self.FAR_S + k],
            self.sems.at[self.FAR_R + k],
            (p.far, p.core),
        )

    def copy_near(self, z):
        p = self.place
        return send(
            self.at(self.far, z * 2 + 1 - p.near_bit),
            self.at(self.near, z),
            self.sems.at[self.NEAR_S + z],
            self.sems.at[self.NEAR_R + z],
            (p.near, p.core),
        )

    def copy_up(self, z):
        p = self.place
        return send(
            self.at(self.near, z),
            self.at(self.low, z),
            self.sems.at[self.UP_S + z],
            self.sems.at[self.UP_R + z],
            (p.me + 4, p.core),
        )

    def copy_down(self, z):
        p = self.place
        return send(
            self.at(self.near, z),
            self.at(self.high, z),
            self.sems.at[self.DOWN_S + z],
            self.sems.at[self.DOWN_R + z],
            (p.me - 4, p.core),
        )

    def copy_last(self):
        p = self.place
        return send(
            self.own,
            self.out.at[:, self.columns(p.core)],
            self.sems.at[self.LAST_S],
            self.sems.at[self.LAST_R],
            p.partner(),
        )

    def start(self):
        self.copy_local().start()
        self.copy_pair().start()

    def to_far(self):
        p = self.place
        self.copy_local().wait()
        self.copy_pair().wait_recv()

        @pl.loop(0, 8)
        def _(k):
            q = p.chip(k // 2, 1 - p.far_bit, k % 2)
            self.store(self.mine, q, self.load(self.mine, q) + self.load(self.pair, q))
            self.copy_far(k).start()

    def to_near(self):
        p = self.place

        def add(k):
            q = p.chip(k // 2, p.far_bit, k % 2)
            self.copy_far(k).wait_recv()
            self.store(
                self.far, k, self.load(self.far, k) + self.load(self.mine, q) + self.load(self.pair, q)
            )

        @pl.loop(0, 4)
        def _(z):
            add(z * 2 + 1 - p.near_bit)
            self.copy_near(z).start()

        @pl.loop(0, 4)
        def _(z):
            add(z * 2 + p.near_bit)

    def to_line(self):
        p = self.place

        @pl.loop(0, 4)
        def _(z):
            self.copy_near(z).wait_recv()
            self.store(self.near, z, self.load(self.near, z) + self.load(self.far, z * 2 + p.near_bit))

        @pl.when(p.z == 0)
        def _():
            for z in (3, 2, 1):
                self.copy_up(z).start()

        @pl.when(p.z == ZS - 1)
        def _():
            for z in (0, 1, 2):
                self.copy_down(z).start()

    def along(self, step):
        p = self.place

        @pl.when(p.z == step)
        def _():
            for z in (3, 2, 1):
                if z >= step:
                    self.copy_up(z).wait_recv()
                if z > step:
                    self.store(self.near, z, self.load(self.near, z) + self.load(self.low, z))
                    self.copy_up(z).start()

        @pl.when(p.z == ZS - 1 - step)
        def _():
            for z in (0, 1, 2):
                if z <= ZS - 1 - step:
                    self.copy_down(z).wait_recv()
                if z < ZS - 1 - step:
                    self.store(self.near, z, self.load(self.near, z) + self.load(self.high, z))
                    self.copy_down(z).start()

    def to_last(self):
        p = self.place
        self.own[...] = self.load(self.near, p.z)

        @pl.when(p.z > 0)
        def _():
            self.own[...] += self.load(self.low, p.z)

        @pl.when(p.z < ZS - 1)
        def _():
            self.own[...] += self.load(self.high, p.z)

        self.copy_last().start()
        self.out[:, self.columns(p.core)] = self.own[...]

    def finish(self):
        p = self.place
        self.copy_pair().wait_send()

        @pl.loop(0, 8)
        def _(k):
            self.copy_far(k).wait_send()

        @pl.loop(0, 4)
        def _(z):
            self.copy_near(z).wait_send()

            @pl.when(z > p.z)
            def _():
                self.copy_up(z).wait_send()

            @pl.when(z < p.z)
            def _():
                self.copy_down(z).wait_send()

        self.copy_last().wait()

    def stages(self):
        return [
            self.start,
            self.to_far,
            self.to_near,
            self.to_line,
            lambda: self.along(1),
            lambda: self.along(2),
            lambda: self.along(3),
            self.to_last,
            self.finish,
        ]

    @staticmethod
    def scratch(shape):
        total, cols = shape[0], shape[1] // 2
        rows = total // 16
        return [
            pltpu.VMEM((total, cols), half),
            pltpu.VMEM((total, cols), half),
            pltpu.VMEM((8 * rows, cols), half),
            pltpu.VMEM((4 * rows, cols), half),
            pltpu.VMEM((4 * rows, cols), half),
            pltpu.VMEM((4 * rows, cols), half),
            pltpu.VMEM((rows, cols), single),
            pltpu.SemaphoreType.DMA((Scatter.COUNT,)),
        ]


def scatter_body(count, *refs):
    grads, outs = refs[:count], refs[count : 2 * count]
    rest = refs[2 * count :]
    place = Place()
    sem, expect = place.barrier()
    runs = []
    for t in range(count):
        rows = grads[t].shape[0] // 16
        runs.append(Scatter(place, grads[t], rows, outs[t], *rest[8 * t : 8 * t + 8]))
    pl.semaphore_wait(sem, expect)
    table = [run.stages() for run in runs]
    for wave in range(count + len(table[0]) - 1):
        for t in range(count):
            if 0 <= wave - t < len(table[t]):
                table[t][wave - t]()


def scatter_sum(grads, collective_id):
    count = len(grads)
    outs = [jax.ShapeDtypeStruct((g.shape[0] // 16, g.shape[1]), single) for g in grads]
    return pl.pallas_call(
        functools.partial(scatter_body, count),
        in_specs=[pl.BlockSpec(memory_space=pl.ANY)] * count,
        out_specs=[pl.BlockSpec(memory_space=pltpu.VMEM)] * count,
        out_shape=outs,
        scratch_shapes=sum([Scatter.scratch(g.shape) for g in grads], []),
        compiler_params=pltpu.CompilerParams(
            collective_id=collective_id, has_side_effects=True, vmem_limit_bytes=VMEM_LIMIT
        ),
        name=f"scatter_{collective_id}",
    )(*grads)


def small_body(blocks_ref, out_ref, got, send_sem, recv_sem):
    me = lax.axis_index("dp")
    core = lax.axis_index("rep")
    sem = pltpu.get_barrier_semaphore()
    total = 32
    mine = me * 2 + core

    @pl.loop(0, total)
    def _(d):
        @pl.when(d != mine)
        def _():
            pl.semaphore_signal(sem, inc=1, device_id=(d // 2, d % 2), device_id_type=MESH)

    pl.semaphore_wait(sem, total - 1)

    def copy(d):
        return send(blocks_ref.at[d // 2], got.at[mine], send_sem.at[d], recv_sem.at[mine], (d // 2, d % 2))

    @pl.loop(0, total)
    def _(d):
        pl.when(d != mine)(lambda: copy(d).start())

    got[mine] = blocks_ref[me]

    @pl.loop(0, total)
    def _(d):
        @pl.when(d != mine)
        def _():
            copy(d).wait_send()
            send(got.at[d], got.at[d], send_sem.at[d], recv_sem.at[d], (d // 2, d % 2)).wait_recv()

    out_ref[...] = jnp.sum(got[...], axis=0)


def small_sum(blocks, collective_id):
    _, rows, lanes = blocks.shape
    return pl.pallas_call(
        small_body,
        in_specs=[pl.BlockSpec(memory_space=pltpu.VMEM)],
        out_specs=pl.BlockSpec(memory_space=pltpu.VMEM),
        out_shape=jax.ShapeDtypeStruct((rows, lanes), single),
        scratch_shapes=[
            pltpu.VMEM((32, rows, lanes), single),
            pltpu.SemaphoreType.DMA((32,)),
            pltpu.SemaphoreType.DMA((32,)),
        ],
        compiler_params=pltpu.CompilerParams(collective_id=collective_id, has_side_effects=True),
        name=f"small_{collective_id}",
    )(blocks)


def pack_small(vectors, b_up, low):
    n = vectors[0].shape[0]
    block = jnp.concatenate([jnp.stack(vectors), b_up.reshape(-1, n)])
    block = lax.reduce_precision(block, 8, 7) if low else block
    return jnp.pad(block, ((0, 16 - block.shape[0]), (0, 128 - n)))


def unpack_small(full, chips, n):
    full = full.reshape(chips, 16, 128)
    vectors = full[:, :8, :n].transpose(1, 0, 2).reshape(8, chips * n)
    return vectors, full[:, 8:12, :n].reshape(1, 4 * chips * n)


def local(chips, twins, tokens, flags, mask_embed, cotangent, w_qkv, b_qv, w_out, b_out, norm_one, w_up, b_up, w_down, b_down, norm_two):
    own_kernels = chips == 16 and twins == 2
    n = b_out.shape[0]
    width = chips * n
    small = pack_small(
        [b_qv[0], b_qv[1], b_out, norm_one[0], norm_one[1], b_down, norm_two[0], norm_two[1]], b_up, True
    )
    shards = [w_qkv, w_out, w_up, w_down]
    if own_kernels:
        *fulls, small_full = gather_all(shards + [small], [half] * 4 + [single], 1)
    else:
        fulls = [lax.all_gather(s.astype(half), "dp", axis=0, tiled=True) for s in shards]
        small_full = lax.all_gather(small, "dp", axis=0, tiled=True)
    qkv_full, out_full, up_full, down_full = fulls
    vecs, bup_full = unpack_small(small_full, chips, n)
    bias = jnp.concatenate([vecs[0], jnp.zeros_like(vecs[0]), vecs[1]])[None]
    flag_col = flags[:, None]
    inputs, projected = project(tokens, flag_col, mask_embed[None], qkv_full, bias)
    mixed, logs = attend(projected)
    activations, d_sum, d_mixed, g_small, g_bup, g_out, g_up, g_down = middle(
        mixed, inputs, flag_col, cotangent, vecs, bup_full, out_full, up_full, down_full
    )
    d_parts = attend_back(projected, d_mixed, mixed, logs)
    g_qkv, sums = weight_back(inputs, d_parts)
    input_grad = input_back(d_parts, qkv_full, d_sum, flag_col)
    g_small = jnp.concatenate([sums[0:1, :width], sums[0:1, 2 * width :], g_small[2:8]])
    g_small = g_small.reshape(8, chips, n).transpose(1, 0, 2)
    g_small = jnp.concatenate([g_small, g_bup.reshape(chips, 4, n)], axis=1)
    g_small = jnp.pad(g_small, ((0, 0), (0, 4), (0, 128 - n)))
    grads = [g_qkv, g_out, g_up, g_down]
    if own_kernels:
        grads = scatter_sum(grads, 2)
        g_small = small_sum(g_small, 3)
    else:
        grads = [lax.psum_scatter(g.astype(single), "dp", scatter_dimension=0, tiled=True) for g in grads]
        grads = [lax.psum(g.astype(half), "rep").astype(single) for g in grads]
        g_small = lax.psum_scatter(g_small, "dp", scatter_dimension=0, tiled=False)
        g_small = lax.psum(g_small, "rep")
    g_qkv, g_out, g_up, g_down = grads
    rows = g_small[:, :n]
    return (
        activations,
        input_grad,
        g_qkv,
        rows[0:2],
        g_out,
        rows[2],
        rows[3:5],
        g_up,
        rows[8:12].reshape(4 * n),
        g_down,
        rows[5],
        rows[6:8],
    )


def solution(mesh):
    rows = P(("dp", "rep"), None)
    first = P("dp", None)
    second = P(None, "dp")
    return jax.shard_map(
        functools.partial(local, mesh.shape["dp"], mesh.shape["rep"]),
        mesh=mesh,
        in_specs=(rows, P(("dp", "rep")), P(), rows, first, second, first, P("dp"), second, first, P("dp"), first, P("dp"), second),
        out_specs=(rows, rows, first, second, first, P("dp"), second, first, P("dp"), first, P("dp"), second),
        check_vma=False,
    )
```

time: 1630 us -> 430 us (0.26)
  waiting for transfers between devices: 780 us -> 0 us
  Pallas kernels: 0 us -> 407 us
  matrix products: 337 us -> 0 us
  blocking collectives: 267 us -> 0 us
  other arithmetic: 119 us -> 1.39 us
  local copies, waits for them, and re-layouts: 101 us -> 17.8 us
  between operations: 17.9 us -> 0.78 us
    reduce_scatter x4 -> x0, waiting for transfers between devices: 485 us -> none  [the longest x1 175 us: local(): lax.psum_scatter(grad_w_down, 'dp', scatter_dimension=0, tiled=True)]
    pallas_call x0 -> x9, Pallas kernels: none -> 407 us  [the longest x1 108 us: middle(): pl.pallas_call(middle_body, grid=(count // block,), in_specs=[rows(width)...]
    dot_general x18 -> x0, matrix products: 337 us -> none  [the longest x1 64.7 us: local(): jnp.dot(first_low, up_full, preferred_element_type=single)]
    unnamed x15 -> x0, waiting for transfers between devices: 280 us -> none
    unnamed x2 -> x0, blocking collectives: 155 us -> none
    all_gather x3 -> x0, blocking collectives: 110 us -> none  [the longest x1 37.6 us: local(): lax.all_gather(norm_one.astype(half), 'dp', axis=1, tiled=True)]
    convert_element_type x29 -> x0, other arithmetic: 69.1 us -> none  [the longest x1 41.3 us: local(): (probs * (d_probs - jnp.sum(d_probs * probs, axis=-1, keepdims=True))).as...]
    reduce_sum x7 -> x0, other arithmetic: 46.1 us -> none  [the longest x1 20.1 us: local(): total = jnp.sum(expo, axis=-1, keepdims=True)]
  transfers between devices with their start and end apart: 12 -> 0, of which waited for: 7 -> 0; matrix products, arithmetic and copies ran while one was open for 23% -> 0% of each run, Pallas kernels for 0% -> 0%
where the time goes in v1:
time: 430 us; the launch traced here: 427 us
  Pallas kernels  407 us (95%)
  local copies, waits for them, and re-layouts  17.8 us (4%)
    pallas_call x1, Pallas kernels, middle(): pl.pallas_call(middle_body, grid=(count // block,), in_specs=[rows(width)...  108 us
    pallas_call x1, Pallas kernels, scatter_sum(): pl.pallas_call(functools.partial(scatter_body, count), in_specs=[pl.Block...  94.6 us
    pallas_call x1, Pallas kernels, gather_all(): pl.pallas_call(functools.partial(gather_body, count), in_specs=[pl.BlockS...  81.4 us
    pallas_call x1, Pallas kernels, attend_back(): pl.pallas_call(functools.partial(attend_back_body, pairs), grid=(groups,...  39.6 us
    pallas_call x1, Pallas kernels, attend(): pl.pallas_call(functools.partial(attend_body, pairs), grid=(groups, steps...  28.6 us
    pallas_call x1, Pallas kernels, input_back(): pl.pallas_call(input_back_body, grid=(count // block,), in_specs=[spec] *...  15.4 us
    pallas_call x1, Pallas kernels, weight_back(): pl.pallas_call(weight_back_body, grid=(3, steps), in_specs=[pl.BlockSpec(...  14.4 us
    pallas_call x1, Pallas kernels, project(): pl.pallas_call(project_body, grid=(count // block,), in_specs=[pl.BlockSp...  13.6 us

profile of v1, /device:TPU:0, one launch (start us, length us, event | category | flops | bytes accessed | tf_op | source)
XLA Modules:
  0.0 427.1 jit_solution(4365496413849963363)
XLA Ops:
  0.6 0.8 reshape.49
  1.4 0.8 concatenate.13
  2.8 81.4 %gather_1.1 = (bf16[768,2304]{1,0:T(8,128)(2,1)}, bf16[768,768]{1,0:T(8,128)(2,1)}, bf16[768,3072]{1,0:T(8,128)(2,1)}, bf16[3072,768]{1,0:T(8,128)(2,1)}, f32[256,128]{1,0:T(8,128)}) custom-call(f32[48,2304]{1,0:T(8,128)} %refs_0_.1, f32[48,768]{1,0:T(8,128)} %refs_1_.1, f32[48,3072]{1,0:T(8,128)} %refs_2_.1, f32[192,768]{1,0:T(8,128)} %refs_3_.1, ...), custom_call_target="tpu_custom_call" | custom-call | tf_op jit(solution)/shard_map/gather_1/pallas_call | solution.py:610
  84.2 0.8 slice_bitcast_fusion
  85.8 2.0 copy.27.flag_ref
  87.8 1.3 broadcast_in_dim.13.mask_ref
  89.1 13.6 %project.1 = (bf16[2048,768]{1,0:T(8,128)(2,1)}, bf16[2048,2304]{1,0:T(8,128)(2,1)}) custom-call(bf16[2048,768]{1,0:T(8,128)(2,1)} %tok_ref.1, s32[2048,1]{1,0:T(8,128)} %copy.27.flag_ref, bf16[1,768]{1,0:T(2,128)(2,1)} %broadcast_in_dim.13.mask_ref, bf16[768,2304]{1,0:T(8,128)(2,1)} %get-tuple-element.38.w_ref, f32[1,2304]{1,0:T(1,128)} %broadcast_in_dim.15.bias_ref), custom_call_target="tpu_custom_call" | custom-call | tf_op jit(solution)/shard_map/project/pallas_call | solution.py:50
  102.7 28.6 %attend.1 = (bf16[2048,768]{1,0:T(8,128)(2,1)}, f32[4,3,8,512]{3,2,1,0:T(8,128)}) custom-call(bf16[2048,2304]{1,0:T(8,128)(2,1)} %get-tuple-element.40.q_ref.k_ref.v_ref, bf16[2048,2304]{1,0:T(8,128)(2,1)} %get-tuple-element.40.q_ref.k_ref.v_ref, bf16[2048,2304]{1,0:T(8,128)(2,1)} %get-tuple-element.40.q_ref.k_ref.v_ref), custom_call_target="tpu_custom_call" | custom-call | tf_op jit(solution)/shard_map/attend/pallas_call | solution.py:109
  131.4 0.7 reshape.51.vec_ref
  132.1 0.8 slice.73
  132.9 0.7 reshape.52.bup_ref
  133.6 108.1 %middle.1 = (bf16[2048,768]{1,0:T(8,128)(2,1)}, f32[2048,768]{1,0:T(8,128)}, bf16[2048,768]{1,0:T(8,128)(2,1)}, f32[8,768]{1,0:T(8,128)}, f32[1,3072]{1,0:T(1,12...) custom-call(bf16[2048,768]{1,0:T(8,128)(2,1)} %get-tuple-element.41.mixed_ref, ...), custom_call_target="tpu_custom_call" | custom-call | tf_op jit(solution)/shard_map/middle/pallas_call | solution.py:320
  241.8 39.6 %attend_back.1 = (bf16[2048,768]{1,0:T(8,128)(2,1)}, bf16[2048,768]{1,0:T(8,128)(2,1)}, bf16[2048,768]{1,0:T(8,128)(2,1)}) custom-call(bf16[2048,2304]{1,0:T(8,128)(2,1)} %get-tuple-element.40.q_ref.k_ref.v_ref, bf16[2048,2304]{1,0:T(8,128)(2,1)} %get-tuple-element.40.q_ref.k_ref.v_ref, bf16[2048,2304]{1,0:T(8,128)(2,1)} %get-tuple-element.40.q_ref.k_ref.v_ref, ...), custom_call_target="tpu_custom_call" | custom-call | tf_op jit(solution)/shard_map/attend_back/pallas_call | solution.py:171
  281.4 14.4 %weight_back.1 = (bf16[768,2304]{1,0:T(8,128)(2,1)}, f32[8,2304]{1,0:T(8,128)}) custom-call(bf16[2048,768]{1,0:T(8,128)(2,1)} %get-tuple-element.42.inp_ref, bf16[2048,768]{1,0:T(8,128)(2,1)} %get-tuple-element.49.dq_ref, bf16[2048,768]{1,0:T(8,128)(2,1)} %get-tuple-element.50.dk_ref, bf16[2048,768]{1,0:T(8,128)(2,1)} %get-tuple-element.51.dv_ref), custom_call_target="tpu_custom_call" | custom-call | tf_op jit(solution)/shard_map/weight_back/pallas_call | solution.py:394
  295.8 0.8 fusion
  298.0 0.7 select_maximum_fusion.blocks_ref
  298.7 11.4 %small_3.1 = f32[16,128]{1,0:T(8,128)} custom-call(f32[16,16,128]{2,1,0:T(8,128)} %select_maximum_fusion.blocks_ref), custom_call_target="tpu_custom_call" | custom-call | tf_op jit(solution)/shard_map/small_3/pallas_call | solution.py:927
  310.1 1.4 fusion.1
  312.7 1.3 slice_bitcast_fusion.1
  314.0 94.6 %scatter_2.1 = (f32[48,2304]{1,0:T(8,128)}, f32[48,768]{1,0:T(8,128)}, f32[48,3072]{1,0:T(8,128)}, f32[192,768]{1,0:T(8,128)}) custom-call(bf16[768,2304]{1,0:T(8,128)(2,1)} %get-tuple-element.53.refs_0_, bf16[768,768]{1,0:T(8,128)(2,1)} %get-tuple-element.54.refs_1_, bf16[768,3072]{1,0:T(8,128)(2,1)} %get-tuple-element.55.refs_2_, ...), custom_call_target="tpu_custom_call" | custom-call | tf_op jit(solution)/shard_map/scatter_2/pallas_call | solution.py:878
  408.6 15.4 %input_back.1 = f32[2048,768]{1,0:T(8,128)} custom-call(bf16[2048,768]{1,0:T(8,128)(2,1)} %get-tuple-element.49.dq_ref, bf16[2048,768]{1,0:T(8,128)(2,1)} %get-tuple-element.50.dk_ref, bf16[2048,768]{1,0:T(8,128)(2,1)} %get-tuple-element.51.dv_ref, bf16[768,2304]{1,0:T(8,128)(2,1)} %get-tuple-element.38.w_ref, f32[2048,768]{1,0:T(8,128)} %get-tuple-element.52.dsum_ref, ...), custom_call_target="tpu_custom_call" | custom-call | tf_op jit(solution)/shard_map/input_back/pallas_call | solution.py:423
  424.1 0.8 copy.38
  425.5 0.8 copy.40
  426.3 0.8 copy.41
  (31 shorter events, 4.8 us)
Async XLA Ops:
  281.4 15.2 %copy-start.4 = (f32[8,768]{1,0:T(8,128)S(1)}, f32[8,768]{1,0:T(8,128)}, u32[]{:S(2)}) copy-start(f32[8,768]{1,0:T(8,128)} %get-tuple-element.59) | copy-start | bytes 73732
  281.4 15.9 %copy-start.5 = (f32[1,3072]{1,0:T(1,128)S(1)}, f32[1,3072]{1,0:T(1,128)}, u32[]{:S(2)}) copy-start(f32[1,3072]{1,0:T(1,128)} %get-tuple-element.60) | copy-start | bytes 36868
  408.6 15.5 %copy-start.2 = (f32[48,2304]{1,0:T(8,128)S(1)}, f32[48,2304]{1,0:T(8,128)}, u32[]{:S(2)}) copy-start(f32[48,2304]{1,0:T(8,128)} %get-tuple-element.87) | copy-start | bytes 1327108
  408.6 16.2 %copy-start.3 = (f32[48,768]{1,0:T(8,128)S(1)}, f32[48,768]{1,0:T(8,128)}, u32[]{:S(2)}) copy-start(f32[48,768]{1,0:T(8,128)} %get-tuple-element.89) | copy-start | bytes 442372
  408.6 16.9 %copy-start.1 = (f32[48,3072]{1,0:T(8,128)S(1)}, f32[48,3072]{1,0:T(8,128)}, u32[]{:S(2)}) copy-start(f32[48,3072]{1,0:T(8,128)} %get-tuple-element.92) | copy-start | bytes 1769476
  408.6 17.7 %copy-start = (f32[192,768]{1,0:T(8,128)S(1)}, f32[192,768]{1,0:T(8,128)}, u32[]{:S(2)}) copy-start(f32[192,768]{1,0:T(8,128)} %get-tuple-element.94) | copy-start | bytes 1769476

commit v2 on v1

--- a/solution.py
+++ b/solution.py
@@ -145,47 +145,6 @@
     return d_query.astype(half), turn(d_keys), turn(d_vals)
 
 
-def attend_back_body(pairs, q_ref, k_ref, v_ref, grad_ref, mixed_ref, log_ref, dq_ref, dk_ref, dv_ref):
-    logs = log_ref[0, 0].T
-    for p in range(pairs):
-        cols = pl.ds(128 * p, 128)
-        dq, dk, dv = attend_back_pair(
-            q_ref[:, cols],
-            k_ref[:, cols],
-            v_ref[:, cols],
-            grad_ref[:, cols],
-            mixed_ref[:, cols],
-            logs[:, 2 * p : 2 * p + 2],
-        )
-        dq_ref[:, cols] = dq
-        dk_ref[:, cols] = dk
-        dv_ref[:, cols] = dv
-
-
-def attend_back(projected, d_mixed, mixed, logs, pairs=2):
-    count, width = mixed.shape
-    groups = count // SEQ
-    steps = width // (128 * pairs)
-    spec = lambda part: pl.BlockSpec((SEQ, 128 * pairs), lambda g, p: (g, part * steps + p))
-    out = pl.BlockSpec((SEQ, 128 * pairs), lambda g, p: (g, p))
-    return pl.pallas_call(
-        functools.partial(attend_back_body, pairs),
-        grid=(groups, steps),
-        in_specs=[
-            spec(0),
-            spec(1),
-            spec(2),
-            out,
-            out,
-            pl.BlockSpec((1, 1, 8, SEQ), lambda g, p: (g, p, 0, 0)),
-        ],
-        out_specs=[out] * 3,
-        out_shape=[jax.ShapeDtypeStruct((count, width), half)] * 3,
-        compiler_params=pltpu.CompilerParams(vmem_limit_bytes=VMEM_LIMIT),
-        name="attend_back",
-    )(projected, projected, projected, d_mixed, mixed, logs)
-
-
 def norm(values, gain, shift):
     center = values - row_mean(values)
     inverse = lax.rsqrt(row_mean(center * center) + EPS)
@@ -212,7 +171,6 @@
     dsum_out,
     dmix_out,
     small_out,
-    gbup_out,
     gwo_out,
     gwu_out,
     gwd_out,
@@ -237,7 +195,6 @@
     @pl.when(step == 0)
     def _():
         small_out[...] = jnp.zeros_like(small_out)
-        gbup_out[...] = jnp.zeros_like(gbup_out)
         acc_o[...] = jnp.zeros_like(acc_o)
         acc_u[...] = jnp.zeros_like(acc_u)
         acc_d[...] = jnp.zeros_like(acc_d)
@@ -276,7 +233,7 @@
         cols = pl.ds(pl.multiple_of(j * width, width), width)
         d_acts = mm_tb(d_low[...], wd_ref[cols, :])
         d_upper = (d_acts * slope[j].astype(single)).astype(half)
-        gbup_out[:, cols] += col_sum(d_upper.astype(single))
+        small_out[pl.ds(8 + j, 1), :] += col_sum(d_upper.astype(single))
         total[...] += mm_tb(d_upper, wu_ref[:, cols])
         acc_d[j] += mm_ta(acts[j], d_low[...])
         acc_u[j] += mm_ta(low[...], d_upper)
@@ -335,8 +292,7 @@
             rows(width),
             rows(width),
             rows(width),
-            keep((8, width)),
-            keep((1, hidden)),
+            keep((16, width)),
             whole,
             whole,
             whole,
@@ -345,8 +301,7 @@
             jax.ShapeDtypeStruct((count, width), half),
             jax.ShapeDtypeStruct((count, width), single),
             jax.ShapeDtypeStruct((count, width), half),
-            jax.ShapeDtypeStruct((8, width), single),
-            jax.ShapeDtypeStruct((1, hidden), single),
+            jax.ShapeDtypeStruct((16, width), single),
             jax.ShapeDtypeStruct((width, width), half),
             jax.ShapeDtypeStruct((width, hidden), half),
             jax.ShapeDtypeStruct((hidden, width), half),
@@ -370,72 +325,6 @@
     )(mixed, inputs, flags, cotangent, vecs, b_up, w_out, w_up, w_down)
 
 
-def weight_back_body(inp_ref, dq_ref, dk_ref, dv_ref, out_ref, sum_ref):
-    part = pl.program_id(0)
-
-    def work(ref):
-        grad = ref[...]
-        out_ref[...] = mm_ta(inp_ref[...], grad).astype(half)
-        sum_ref[...] = jnp.broadcast_to(col_sum(grad.astype(single)), sum_ref.shape)
-
-    for n, ref in enumerate((dq_ref, dk_ref, dv_ref)):
-        pl.when(part == n)(functools.partial(work, ref))
-
-
-def weight_back(inputs, d_parts, block=256):
-    count, width = inputs.shape
-    steps = width // block
-
-    def spec(n):
-        return pl.BlockSpec(
-            (count, block), lambda p, i: (0, jnp.where(p == n, i, jnp.where(p > n, steps - 1, 0)))
-        )
-
-    return pl.pallas_call(
-        weight_back_body,
-        grid=(3, steps),
-        in_specs=[pl.BlockSpec((count, width), lambda p, i: (0, 0), pipeline_mode=pl.Buffered(1))]
-        + [spec(n) for n in range(3)],
-        out_specs=[
-            pl.BlockSpec((width, block), lambda p, i: (0, p * steps + i)),
-            pl.BlockSpec((8, block), lambda p, i: (0, p * steps + i)),
-        ],
-        out_shape=[
-            jax.ShapeDtypeStruct((width, 3 * width), half),
-            jax.ShapeDtypeStruct((8, 3 * width), single),
-        ],
-        compiler_params=pltpu.CompilerParams(vmem_limit_bytes=VMEM_LIMIT),
-        name="weight_back",
-    )(inputs, *d_parts)
-
-
-def input_back_body(dq_ref, dk_ref, dv_ref, w_ref, dsum_ref, flag_ref, out_ref):
-    width = dq_ref.shape[1]
-    grad = dsum_ref[...]
-    for part, ref in enumerate((dq_ref, dk_ref, dv_ref)):
-        grad = grad + mm_tb(ref[...], w_ref[:, pl.ds(part * width, width)])
-    out_ref[...] = jnp.where(flag_ref[...] > 0, 0.0, grad)
-
-
-def input_back(d_parts, w_qkv, d_sum, flags, block=256):
-    count, width = d_sum.shape
-    spec = pl.BlockSpec((block, width), lambda i: (i, 0))
-    return pl.pallas_call(
-        input_back_body,
-        grid=(count // block,),
-        in_specs=[spec] * 3
-        + [
-            pl.BlockSpec(w_qkv.shape, lambda i: (0, 0), pipeline_mode=pl.Buffered(1)),
-            spec,
-            pl.BlockSpec((block, 1), lambda i: (i, 0)),
-        ],
-        out_specs=spec,
-        out_shape=jax.ShapeDtypeStruct((count, width), single),
-        compiler_params=pltpu.CompilerParams(vmem_limit_bytes=VMEM_LIMIT),
-        name="input_back",
-    )(*d_parts, w_qkv, d_sum, flags)
-
-
 MESH = pl.DeviceIdType.MESH
 ZS = 4
 
@@ -468,15 +357,9 @@
         tell((self.near, self.core))
         tell((self.far, self.core))
 
-        @pl.when(self.z > 0)
-        def _():
-            tell((self.me - 4, self.core))
-
-        @pl.when(self.z < ZS - 1)
-        def _():
-            tell((self.me + 4, self.core))
-
-        return sem, 3 + jnp.minimum(self.z, 1) + jnp.minimum(ZS - 1 - self.z, 1)
+        for k in range(1, ZS):
+            tell(((self.me + 4 * k) % (4 * ZS), self.core))
+        return sem, 3 + ZS - 1
 
 
 def send(src, dst, send_sem, recv_sem, dev):
@@ -627,10 +510,10 @@
 
 
 class Scatter:
-    def __init__(self, place, grad, rows, out, mine, pair, far, near, low, high, own, sems):
+    def __init__(self, place, grad, rows, out, mine, pair, far, near, low, high, own, got, sems):
         self.place = place
         self.grad, self.rows, self.out = grad, rows, out
-        self.mine, self.pair, self.far, self.near, self.low, self.high, self.own = mine, pair, far, near, low, high, own
+        self.mine, self.pair, self.far, self.near, self.low, self.high, self.own, self.got = mine, pair, far, near, low, high, own, got
         self.sems = sems
         self.cols = grad.shape[1] // 2
 
@@ -710,7 +593,7 @@
         p = self.place
         return send(
             self.own,
-            self.out.at[:, self.columns(p.core)],
+            self.got,
             self.sems.at[self.LAST_S],
             self.sems.at[self.LAST_R],
             p.partner(),
@@ -825,6 +708,7 @@
                 self.copy_down(z).wait_send()
 
         self.copy_last().wait()
+        self.out[:, self.columns(1 - p.core)] = self.got[...]
 
     def stages(self):
         return [
@@ -851,92 +735,265 @@
             pltpu.VMEM((4 * rows, cols), half),
             pltpu.VMEM((4 * rows, cols), half),
             pltpu.VMEM((rows, cols), single),
+            pltpu.VMEM((rows, cols), single),
             pltpu.SemaphoreType.DMA((Scatter.COUNT,)),
         ]
 
 
-def scatter_body(count, *refs):
-    grads, outs = refs[:count], refs[count : 2 * count]
-    rest = refs[2 * count :]
-    place = Place()
-    sem, expect = place.barrier()
-    runs = []
-    for t in range(count):
-        rows = grads[t].shape[0] // 16
-        runs.append(Scatter(place, grads[t], rows, outs[t], *rest[8 * t : 8 * t + 8]))
-    pl.semaphore_wait(sem, expect)
-    table = [run.stages() for run in runs]
-    for wave in range(count + len(table[0]) - 1):
-        for t in range(count):
-            if 0 <= wave - t < len(table[t]):
-                table[t][wave - t]()
-
-
-def scatter_sum(grads, collective_id):
-    count = len(grads)
-    outs = [jax.ShapeDtypeStruct((g.shape[0] // 16, g.shape[1]), single) for g in grads]
+class Total:
+    COUNT = 12
+
+    def __init__(self, place, start, pair, result, parts, held, sems):
+        self.place, self.first, self.pair, self.result = place, start, pair, result
+        self.parts, self.held, self.sems = parts, held, sems
+
+    def copy(self, n):
+        p = self.place
+        if n == 0:
+            src, dev = self.first, p.partner()
+        elif n <= 3:
+            src, dev = self.held.at[0], ((p.me + 4 * n) % (4 * ZS), p.core)
+        elif n == 4:
+            src, dev = self.held.at[1], (p.near, p.core)
+        else:
+            src, dev = self.held.at[2], (p.far, p.core)
+        return send(src, self.parts.at[n], self.sems.at[n], self.sems.at[6 + n], dev)
+
+    def stages(self):
+        def begin():
+            if self.pair:
+                self.copy(0).start()
+
+        def column():
+            value = self.first[...]
+            if self.pair:
+                self.copy(0).wait_recv()
+                value = value + self.parts[0]
+            self.held[0] = value
+            for n in (1, 2, 3):
+                self.copy(n).start()
+
+        def near():
+            value = self.held[0]
+            for n in (1, 2, 3):
+                self.copy(n).wait_recv()
+                value = value + self.parts[n]
+            self.held[1] = value
+            self.copy(4).start()
+
+        def far():
+            self.copy(4).wait_recv()
+            self.held[2] = self.held[1] + self.parts[4]
+            self.copy(5).start()
+
+        def finish():
+            self.copy(5).wait_recv()
+            self.result[...] = self.held[2] + self.parts[5]
+            for n in range(0 if self.pair else 1, 6):
+                self.copy(n).wait_send()
+
+        return [begin, column, near, far, finish]
+
+    @staticmethod
+    def scratch(shape):
+        return [
+            pltpu.VMEM((6,) + shape, single),
+            pltpu.VMEM((3,) + shape, single),
+            pltpu.SemaphoreType.DMA((Total.COUNT,)),
+        ]
+
+
+PAIRS = 2
+
+
+def back_body(links, plan, *refs):
+    q_ref, k_ref, v_ref, grad_ref, mixed_ref, log_ref, inp_ref, w_ref, dsum_ref, flag_ref, small_ref = refs[:11]
+    rest = refs[11:]
+    step = pl.program_id(0)
+    width = inp_ref.shape[1]
+    count = inp_ref.shape[0]
+    wide = 128 * PAIRS
+    per_group = width // wide
+    attends = (count // SEQ) * per_group
+    weights = 3 * (width // 256)
+    actions = {}
+
+    if links:
+        grads, (out_ref, g_qkv, g_out, g_up, g_down, total_ref) = rest[:3], rest[3:9]
+        parts_ref, made, sums, fixed = rest[9], rest[10], rest[11], rest[12:]
+        place = Place()
+        runs = []
+        sources = [(grads[2], g_down), (grads[1], g_up), (grads[0], g_out)]
+        sources += [(made.at[n], g_qkv.at[:, pl.ds(n * width, width)]) for n in range(3)]
+        for n, (src, dst) in enumerate(sources):
+            runs.append(Scatter(place, src, src.shape[0] // 16, dst, *fixed[9 * n : 9 * n + 9]))
+        runs.append(Total(place, sums, True, total_ref, *fixed[9 * len(sources) :]))
+
+        def enter():
+            sem, expect = place.barrier()
+            pl.semaphore_wait(sem, expect)
+
+        actions.setdefault((0, 0), []).append(enter)
+        for n, run in enumerate(runs):
+            for stage, when in zip(run.stages(), plan[n]):
+                actions.setdefault(when, []).append(stage)
+    else:
+        out_ref, made, total_ref = rest[:3]
+        parts_ref, sums = rest[3:]
+
+    def talk(point):
+        for (at, where), todo in sorted(actions.items(), key=lambda item: item[0]):
+            if where == point:
+
+                def run_all(todo=todo):
+                    for action in todo:
+                        action()
+
+                pl.when(step == at)(run_all)
+
+    @pl.when(step == 0)
+    def _():
+        sums[...] = small_ref[...]
+
+    talk(0)
+
+    @pl.when(step < attends)
+    def _():
+        group = step // per_group
+        column = step % per_group
+        rows = pl.ds(pl.multiple_of(group * SEQ, SEQ), SEQ)
+        logs = log_ref[0, 0].T
+        for p in range(PAIRS):
+            cols = pl.ds(128 * p, 128)
+            done = attend_back_pair(
+                q_ref[:, cols],
+                k_ref[:, cols],
+                v_ref[:, cols],
+                grad_ref[:, cols],
+                mixed_ref[:, cols],
+                logs[:, 2 * p : 2 * p + 2],
+            )
+            where = pl.ds(pl.multiple_of(column * wide + 128 * p, 128), 128)
+            for n in range(3):
+                parts_ref[n, rows, where] = done[n]
+            if p + 1 < PAIRS:
+                talk(1)
+
+    @pl.when((step >= attends) & (step < attends + weights))
+    def _():
+        part = (step - attends) // (width // 256)
+        cols = pl.ds(pl.multiple_of((step - attends) % (width // 256) * 256, 256), 256)
+        grad = parts_ref[part, :, cols]
+        made[part, :, cols] = mm_ta(inp_ref[...], grad).astype(half)
+        column = col_sum(grad.astype(single))
+
+        @pl.when(part == 0)
+        def _():
+            sums[pl.ds(0, 1), cols] = column
+
+        @pl.when(part == 2)
+        def _():
+            sums[pl.ds(1, 1), cols] = column
+
+    @pl.when(step >= attends + weights)
+    def _():
+        block = out_ref.shape[0]
+        rows = pl.ds(pl.multiple_of((step - attends - weights) * block, block), block)
+        grad = dsum_ref[...]
+        for n in range(3):
+            grad = grad + mm_tb(parts_ref[n, rows, :], w_ref[:, pl.ds(n * width, width)])
+        out_ref[...] = jnp.where(flag_ref[...] > 0, 0.0, grad)
+
+    talk(2)
+    if not links:
+        total_ref[...] = sums[...]
+
+
+def back(links, projected, d_mixed, mixed, logs, inputs, w_qkv, d_sum, flags, small, grads):
+    count, width = mixed.shape
+    groups = count // SEQ
+    wide = 128 * PAIRS
+    per_group = width // wide
+    attends = groups * per_group
+    weights = 3 * (width // 256)
+    block = 256
+    last = attends - 1
+
+    def group_of(s):
+        return jnp.minimum(s, last) // per_group
+
+    def column_of(s):
+        return jnp.minimum(s, last) % per_group
+
+    def late(s):
+        return jnp.maximum(s - attends - weights, 0)
+
+    spec = lambda part: pl.BlockSpec((SEQ, wide), lambda s: (group_of(s), part * per_group + column_of(s)))
+    whole = lambda shape: pl.BlockSpec(shape, lambda s: (0,) * len(shape), pipeline_mode=pl.Buffered(1))
+    anywhere = pl.BlockSpec(memory_space=pl.ANY)
+    in_specs = [
+        spec(0),
+        spec(1),
+        spec(2),
+        spec(0),
+        spec(0),
+        pl.BlockSpec((1, 1, 8, SEQ), lambda s: (group_of(s), column_of(s), 0, 0)),
+        whole(inputs.shape),
+        whole(w_qkv.shape),
+        pl.BlockSpec((block, width), lambda s: (late(s), 0)),
+        pl.BlockSpec((block, 1), lambda s: (late(s), 0)),
+        whole(small.shape),
+    ]
+    out_specs = [pl.BlockSpec((block, width), lambda s: (late(s), 0))]
+    out_shape = [jax.ShapeDtypeStruct((count, width), single)]
+    operands = [projected, projected, projected, d_mixed, mixed, logs, inputs, w_qkv, d_sum, flags, small]
+    dparts = pltpu.VMEM((3, count, width), half)
+    sums = pltpu.VMEM(small.shape, single)
+    plan = None
+    if links:
+        in_specs += [anywhere] * 3
+        operands += grads
+        shapes = [(width // 16, 3 * width)] + [(g.shape[0] // 16, g.shape[1]) for g in grads] + [small.shape]
+        out_specs += [whole(shape) for shape in shapes]
+        out_shape += [jax.ShapeDtypeStruct(shape, single) for shape in shapes]
+        scratch = [dparts, pltpu.VMEM((3, width, width), half), sums]
+        for shape in [grads[2].shape, grads[1].shape, grads[0].shape] + [(width, width)] * 3:
+            scratch += Scatter.scratch(shape)
+        scratch += Total.scratch(small.shape)
+        params = pltpu.CompilerParams(collective_id=2, has_side_effects=True, vmem_limit_bytes=VMEM_LIMIT)
+        plan = back_plan(attends, weights, count // block)
+    else:
+        out_specs += [whole((3, width, width)), whole(small.shape)]
+        out_shape += [jax.ShapeDtypeStruct((3, width, width), half), jax.ShapeDtypeStruct(small.shape, single)]
+        scratch = [dparts, sums]
+        params = pltpu.CompilerParams(vmem_limit_bytes=VMEM_LIMIT)
     return pl.pallas_call(
-        functools.partial(scatter_body, count),
-        in_specs=[pl.BlockSpec(memory_space=pl.ANY)] * count,
-        out_specs=[pl.BlockSpec(memory_space=pltpu.VMEM)] * count,
-        out_shape=outs,
-        scratch_shapes=sum([Scatter.scratch(g.shape) for g in grads], []),
-        compiler_params=pltpu.CompilerParams(
-            collective_id=collective_id, has_side_effects=True, vmem_limit_bytes=VMEM_LIMIT
-        ),
-        name=f"scatter_{collective_id}",
-    )(*grads)
-
-
-def small_body(blocks_ref, out_ref, got, send_sem, recv_sem):
-    me = lax.axis_index("dp")
-    core = lax.axis_index("rep")
-    sem = pltpu.get_barrier_semaphore()
-    total = 32
-    mine = me * 2 + core
-
-    @pl.loop(0, total)
-    def _(d):
-        @pl.when(d != mine)
-        def _():
-            pl.semaphore_signal(sem, inc=1, device_id=(d // 2, d % 2), device_id_type=MESH)
-
-    pl.semaphore_wait(sem, total - 1)
-
-    def copy(d):
-        return send(blocks_ref.at[d // 2], got.at[mine], send_sem.at[d], recv_sem.at[mine], (d // 2, d % 2))
-
-    @pl.loop(0, total)
-    def _(d):
-        pl.when(d != mine)(lambda: copy(d).start())
-
-    got[mine] = blocks_ref[me]
-
-    @pl.loop(0, total)
-    def _(d):
-        @pl.when(d != mine)
-        def _():
-            copy(d).wait_send()
-            send(got.at[d], got.at[d], send_sem.at[d], recv_sem.at[d], (d // 2, d % 2)).wait_recv()
-
-    out_ref[...] = jnp.sum(got[...], axis=0)
-
-
-def small_sum(blocks, collective_id):
-    _, rows, lanes = blocks.shape
-    return pl.pallas_call(
-        small_body,
-        in_specs=[pl.BlockSpec(memory_space=pltpu.VMEM)],
-        out_specs=pl.BlockSpec(memory_space=pltpu.VMEM),
-        out_shape=jax.ShapeDtypeStruct((rows, lanes), single),
-        scratch_shapes=[
-            pltpu.VMEM((32, rows, lanes), single),
-            pltpu.SemaphoreType.DMA((32,)),
-            pltpu.SemaphoreType.DMA((32,)),
-        ],
-        compiler_params=pltpu.CompilerParams(collective_id=collective_id, has_side_effects=True),
-        name=f"small_{collective_id}",
-    )(blocks)
+        functools.partial(back_body, links, plan),
+        grid=(attends + weights + count // block,),
+        in_specs=in_specs,
+        out_specs=out_specs,
+        out_shape=out_shape,
+        scratch_shapes=scratch,
+        compiler_params=params,
+        name="back",
+    )(*operands)
+
+
+def back_plan(attends, weights, inputs):
+    def at(n):
+        if n < 2 * attends:
+            return n // 2, n % 2
+        n -= 2 * attends
+        return (attends + n, 0) if n < weights + inputs else (attends + weights + inputs - 1, 2)
+
+    down = [0, 3, 11, 18, 20, 22, 23, 24, 25]
+    up = [0, 5, 19, 25, 27, 28, 29, 30, 31]
+    out = [0, 6, 21, 26, 28, 29, 30, 31, 32]
+    third = lambda n: [n, n + 1, n + 4, n + 6, n + 8, n + 9, n + 10, n + 11, 99]
+    small = [33, 34, 36, 38, 40]
+    after = 2 * attends
+    table = [down, up, out, third(after + 3), third(after + 6), third(after + 9), small]
+    return [[at(n) for n in row] for row in table]
 
 
 def pack_small(vectors, b_up, low):
@@ -971,27 +1028,24 @@
     flag_col = flags[:, None]
     inputs, projected = project(tokens, flag_col, mask_embed[None], qkv_full, bias)
     mixed, logs = attend(projected)
-    activations, d_sum, d_mixed, g_small, g_bup, g_out, g_up, g_down = middle(
+    activations, d_sum, d_mixed, g_small, g_out, g_up, g_down = middle(
         mixed, inputs, flag_col, cotangent, vecs, bup_full, out_full, up_full, down_full
     )
-    d_parts = attend_back(projected, d_mixed, mixed, logs)
-    g_qkv, sums = weight_back(inputs, d_parts)
-    input_grad = input_back(d_parts, qkv_full, d_sum, flag_col)
-    g_small = jnp.concatenate([sums[0:1, :width], sums[0:1, 2 * width :], g_small[2:8]])
-    g_small = g_small.reshape(8, chips, n).transpose(1, 0, 2)
-    g_small = jnp.concatenate([g_small, g_bup.reshape(chips, 4, n)], axis=1)
-    g_small = jnp.pad(g_small, ((0, 0), (0, 4), (0, 128 - n)))
-    grads = [g_qkv, g_out, g_up, g_down]
+    grads = [g_out, g_up, g_down]
+    input_grad, g_qkv, *summed = back(
+        own_kernels, projected, d_mixed, mixed, logs, inputs, qkv_full, d_sum, flag_col, g_small, grads
+    )
     if own_kernels:
-        grads = scatter_sum(grads, 2)
-        g_small = small_sum(g_small, 3)
+        g_out, g_up, g_down, g_small = summed
     else:
+        g_small = summed[0]
+        grads = [jnp.concatenate([g_qkv[0], g_qkv[1], g_qkv[2]], axis=1)] + grads
         grads = [lax.psum_scatter(g.astype(single), "dp", scatter_dimension=0, tiled=True) for g in grads]
-        grads = [lax.psum(g.astype(half), "rep").astype(single) for g in grads]
-        g_small = lax.psum_scatter(g_small, "dp", scatter_dimension=0, tiled=False)
-        g_small = lax.psum(g_small, "rep")
-    g_qkv, g_out, g_up, g_down = grads
-    rows = g_small[:, :n]
+        g_qkv, g_out, g_up, g_down = [lax.psum(g.astype(half), "rep").astype(single) for g in grads]
+        g_small = lax.psum(g_small, ("dp", "rep"))
+    me = lax.axis_index("dp")
+    rows = lax.dynamic_slice_in_dim(g_small[:8], me * n, n, axis=1)
+    g_bup = lax.dynamic_slice_in_dim(g_small[8:12].reshape(4 * width), me * 4 * n, 4 * n)
     return (
         activations,
         input_grad,
@@ -1001,7 +1055,7 @@
         rows[2],
         rows[3:5],
         g_up,
-        rows[8:12].reshape(4 * n),
+        g_bup,
         g_down,
         rows[5],
         rows[6:8],

time: 430 us -> 380 us (0.88)
  Pallas kernels: 407 us -> 357 us
    pallas_call x5 -> x1, Pallas kernels: 175 us -> 124 us  [back(): pl.pallas_call(functools.partial(back_body, links, plan), grid=(attends +...]
    unnamed x16 -> x13, local copies, waits for them, and re-layouts: 3.08 us -> 9.09 us
where the time goes in v2:
time: 380 us
  Pallas kernels  357 us (94%)
  local copies, waits for them, and re-layouts  21.8 us (6%)
    pallas_call x1, Pallas kernels, back(): pl.pallas_call(functools.partial(back_body, links, plan), grid=(attends +...  124 us
    pallas_call x1, Pallas kernels, middle(): pl.pallas_call(middle_body, grid=(count // block,), in_specs=[rows(width)...  108 us
    pallas_call x1, Pallas kernels, gather_all(): pl.pallas_call(functools.partial(gather_body, count), in_specs=[pl.BlockS...  82.4 us
    pallas_call x1, Pallas kernels, attend(): pl.pallas_call(functools.partial(attend_body, pairs), grid=(groups, steps...  28.6 us
    pallas_call x1, Pallas kernels, project(): pl.pallas_call(project_body, grid=(count // block,), in_specs=[pl.BlockSp...  13.6 us
    unnamed x13, local copies, waits for them, and re-layouts  9.09 us

profile of v2, /device:TPU:0, one launch (start us, length us, event | category | flops | bytes accessed | tf_op | source)
XLA Modules:
  0.0 379.7 jit_solution(2423880113043858369)
XLA Ops:
  0.6 0.8 reshape.43
  1.4 0.8 concatenate.7
  2.2 0.6 pad.4.refs_4_
  2.8 82.4 %gather_1.1 = (bf16[768,2304]{1,0:T(8,128)(2,1)}, bf16[768,768]{1,0:T(8,128)(2,1)}, bf16[768,3072]{1,0:T(8,128)(2,1)}, bf16[3072,768]{1,0:T(8,128)(2,1)}, f32[256,128]{1,0:T(8,128)}) custom-call(f32[48,2304]{1,0:T(8,128)} %refs_0_.1, f32[48,768]{1,0:T(8,128)} %refs_1_.1, f32[48,3072]{1,0:T(8,128)} %refs_2_.1, f32[192,768]{1,0:T(8,128)} %refs_3_.1, ...), custom_call_target="tpu_custom_call" | custom-call | tf_op jit(solution)/shard_map/gather_1/pallas_call | solution.py:493
  85.2 0.8 slice_bitcast_fusion
  86.2 0.6 broadcast_in_dim.15.bias_ref
  86.8 2.1 copy.27.flag_ref.refs_9_
  88.9 1.3 broadcast_in_dim.13.mask_ref
  90.2 13.6 %project.1 = (bf16[2048,768]{1,0:T(8,128)(2,1)}, bf16[2048,2304]{1,0:T(8,128)(2,1)}) custom-call(bf16[2048,768]{1,0:T(8,128)(2,1)} %tok_ref.1, s32[2048,1]{1,0:T(8,128)} %copy.27.flag_ref.refs_9_, bf16[1,768]{1,0:T(2,128)(2,1)} %broadcast_in_dim.13.mask_ref, bf16[768,2304]{1,0:T(8,128)(2,1)} %get-tuple-element.34.w_ref.refs_7_, ...), custom_call_target="tpu_custom_call" | custom-call | tf_op jit(solution)/shard_map/project/pallas_call | solution.py:50
  103.8 28.6 %attend.1 = (bf16[2048,768]{1,0:T(8,128)(2,1)}, f32[4,3,8,512]{3,2,1,0:T(8,128)}) custom-call(bf16[2048,2304]{1,0:T(8,128)(2,1)} %get-tuple-element.36.q_ref.k_ref.v_ref.refs_0_.refs_1_.refs_2_, bf16[2048,2304]{1,0:T(8,128)(2,1)} %get-tuple-element.36.q_ref.k_ref.v_ref.refs_0_.refs_1_.refs_2_, ...), custom_call_target="tpu_custom_call" | custom-call | tf_op jit(solution)/shard_map/attend/pallas_call | solution.py:109
  132.4 0.7 reshape.45.vec_ref
  133.1 0.8 slice.58
  134.0 0.7 reshape.46.bup_ref
  134.7 108.2 %middle.1 = (bf16[2048,768]{1,0:T(8,128)(2,1)}, f32[2048,768]{1,0:T(8,128)}, bf16[2048,768]{1,0:T(8,128)(2,1)}, f32[16,768]{1,0:T(8,128)}, bf16[768,768]{1,0:T(8...) custom-call(bf16[2048,768]{1,0:T(8,128)(2,1)} %get-tuple-element.37.mixed_ref.refs_4_, ...), custom_call_target="tpu_custom_call" | custom-call | tf_op jit(solution)/shard_map/middle/pallas_call | solution.py:277
  242.9 124.4 %back.1 = (f32[2048,768]{1,0:T(8,128)}, f32[48,2304]{1,0:T(8,128)}, f32[48,768]{1,0:T(8,128)}, f32[48,3072]{1,0:T(8,128)}, f32[192,768]{1,0:T(8,128)}, /*index=5*/f32[16,768]{1,0:T(8,128)}) custom-call(bf16[2048,2304]{1,0:T(8,128)(2,1)} %get-tuple-element.36.q_ref.k_ref.v_ref.refs_0_.refs_1_.refs_2_, ...), custom_call_target="tpu_custom_call" | custom-call | tf_op jit(solution)/shard_map/back/pallas_call | solution.py:970
  367.3 0.7 slice.48
  368.2 0.6 fusion
  369.2 0.7 slice.52
  370.0 0.6 dynamic_slice.7
  370.6 6.0 %copy.36 = f32[2048,768]{1,0:T(8,128)} copy(f32[2048,768]{1,0:T(8,128)} %get-tuple-element.76) | data formatting | bytes 12582912
  376.7 0.8 copy.37
  377.4 0.7 copy.38
  378.1 0.8 copy.39
  378.9 0.8 copy.40
  (18 shorter events, 0.8 us)
Async XLA Ops:
  370.6 6.0 %copy-start.2 = (f32[48,2304]{1,0:T(8,128)S(1)}, f32[48,2304]{1,0:T(8,128)}, u32[]{:S(2)}) copy-start(f32[48,2304]{1,0:T(8,128)} %get-tuple-element.77) | copy-start | bytes 1327108
  370.6 6.8 %copy-start.3 = (f32[48,768]{1,0:T(8,128)S(1)}, f32[48,768]{1,0:T(8,128)}, u32[]{:S(2)}) copy-start(f32[48,768]{1,0:T(8,128)} %get-tuple-element.79) | copy-start | bytes 442372
  370.6 7.5 %copy-start.1 = (f32[48,3072]{1,0:T(8,128)S(1)}, f32[48,3072]{1,0:T(8,128)}, u32[]{:S(2)}) copy-start(f32[48,3072]{1,0:T(8,128)} %get-tuple-element.82) | copy-start | bytes 1769476
  370.6 8.3 %copy-start = (f32[192,768]{1,0:T(8,128)S(1)}, f32[192,768]{1,0:T(8,128)}, u32[]{:S(2)}) copy-start(f32[192,768]{1,0:T(8,128)} %get-tuple-element.84) | copy-start | bytes 1769476

commit v3 on v2

--- a/solution.py
+++ b/solution.py
@@ -33,41 +33,6 @@
 
 def col_sum(values):
     return jnp.sum(values, axis=0, keepdims=True)
-
-
-def project_body(tok_ref, flag_ref, mask_ref, w_ref, bias_ref, inp_ref, proj_ref):
-    masked = flag_ref[...] > 0
-    inputs = jnp.where(masked, mask_ref[...].astype(single), tok_ref[...].astype(single))
-    low = inputs.astype(half)
-    inp_ref[...] = low
-    proj_ref[...] = (mm(low, w_ref[...]) + bias_ref[...]).astype(half)
-
-
-def project(tokens, flags, mask_embed, w_qkv, bias):
-    count, width = tokens.shape
-    block = 256
-    wide = w_qkv.shape[1]
-    return pl.pallas_call(
-        project_body,
-        grid=(count // block,),
-        in_specs=[
-            pl.BlockSpec((block, width), lambda i: (i, 0)),
-            pl.BlockSpec((block, 1), lambda i: (i, 0)),
-            pl.BlockSpec((1, width), lambda i: (0, 0)),
-            pl.BlockSpec((width, wide), lambda i: (0, 0), pipeline_mode=pl.Buffered(1)),
-            pl.BlockSpec((1, wide), lambda i: (0, 0)),
-        ],
-        out_specs=[
-            pl.BlockSpec((block, width), lambda i: (i, 0)),
-            pl.BlockSpec((block, wide), lambda i: (i, 0)),
-        ],
-        out_shape=[
-            jax.ShapeDtypeStruct((count, width), half),
-            jax.ShapeDtypeStruct((count, wide), half),
-        ],
-        compiler_params=pltpu.CompilerParams(vmem_limit_bytes=VMEM_LIMIT),
-        name="project",
-    )(tokens, flags, mask_embed, w_qkv, bias)
 
 
 def head_masks(width):
@@ -89,38 +54,6 @@
         outs.append(mixed * (1.0 / total))
         logs.append(top + jnp.log(total))
     return jnp.concatenate(outs, axis=0).astype(half).T, logs
-
-
-def attend_body(pairs, q_ref, k_ref, v_ref, mixed_ref, log_ref):
-    for p in range(pairs):
-        cols = pl.ds(128 * p, 128)
-        mixed, logs = attend_pair(q_ref[:, cols], k_ref[:, cols], v_ref[:, cols])
-        mixed_ref[:, cols] = mixed
-        for h in range(2):
-            log_ref[0, 0, pl.ds(2 * p + h, 1), :] = logs[h]
-
-
-def attend(projected, pairs=2):
-    count = projected.shape[0]
-    width = projected.shape[1] // 3
-    groups = count // SEQ
-    steps = width // (128 * pairs)
-    spec = lambda part: pl.BlockSpec((SEQ, 128 * pairs), lambda g, p: (g, part * steps + p))
-    return pl.pallas_call(
-        functools.partial(attend_body, pairs),
-        grid=(groups, steps),
-        in_specs=[spec(0), spec(1), spec(2)],
-        out_specs=[
-            pl.BlockSpec((SEQ, 128 * pairs), lambda g, p: (g, p)),
-            pl.BlockSpec((1, 1, 8, SEQ), lambda g, p: (g, p, 0, 0)),
-        ],
-        out_shape=[
-            jax.ShapeDtypeStruct((count, width), half),
-            jax.ShapeDtypeStruct((groups, steps, 8, SEQ), single),
-        ],
-        compiler_params=pltpu.CompilerParams(vmem_limit_bytes=VMEM_LIMIT),
-        name="attend",
-    )(projected, projected, projected)
 
 
 def attend_back_pair(query, keys, vals, grad, mixed, logs):
@@ -163,7 +96,6 @@
     flag_ref,
     cot_ref,
     vec_ref,
-    bup_ref,
     wo_ref,
     wu_ref,
     wd_ref,
@@ -210,7 +142,7 @@
     @pl.loop(0, chunks)
     def _(j):
         cols = pl.ds(pl.multiple_of(j * width, width), width)
-        upper = mm(low[...], wu_ref[:, cols]) + bup_ref[:, cols]
+        upper = mm(low[...], wu_ref[:, cols]) + vec(8 + j)
         phi = 0.5 * (1.0 + lax.erf(upper * 0.7071067811865476))
         act = (upper * phi).astype(half)
         acts[j] = act
@@ -266,7 +198,7 @@
             copy.wait()
 
 
-def middle(mixed, inputs, flags, cotangent, vecs, b_up, w_out, w_up, w_down, block=512):
+def middle(mixed, inputs, flags, cotangent, vecs, w_out, w_up, w_down, block=512):
     count, width = mixed.shape
     hidden = w_up.shape[1]
     chunks = hidden // width
@@ -282,8 +214,7 @@
             rows(width),
             rows(1),
             rows(width),
-            keep((8, width)),
-            keep((1, hidden)),
+            keep((16, width)),
             once((width, width)),
             once((width, hidden)),
             once((hidden, width)),
@@ -322,7 +253,7 @@
         ],
         compiler_params=pltpu.CompilerParams(vmem_limit_bytes=VMEM_LIMIT),
         name="middle",
-    )(mixed, inputs, flags, cotangent, vecs, b_up, w_out, w_up, w_down)
+    )(mixed, inputs, flags, cotangent, vecs, w_out, w_up, w_down)
 
 
 MESH = pl.DeviceIdType.MESH
@@ -368,23 +299,23 @@
     )
 
 
+OWN, COLUMN, NEAR, FAR, DIAG, END = range(6)
+
+
 class Gather:
-    def __init__(self, place, fulls, rows, sends, recvs, passed):
-        self.place = place
-        self.fulls = fulls
-        self.rows = rows
+    def __init__(self, place, own, full, rows, offset, cols, sends, recvs, passed):
+        self.place, self.own, self.full = place, own, full
+        self.rows, self.offset, self.cols = rows, offset, cols
+        self.stride = full.shape[1] // 2
         self.sends, self.recvs, self.passed = sends, recvs, passed
 
-    def piece(self, t, q, h):
-        full = self.fulls[t]
-        rows = self.rows[t]
-        if full.shape[1] == 128:
-            part = rows // 2
-            return full.at[pl.ds(pl.multiple_of(q * rows + h * part, 8), part), :]
-        cols = full.shape[1] // 2
-        return full.at[pl.ds(pl.multiple_of(q * rows, 16), rows), pl.ds(pl.multiple_of(h * cols, 128), cols)]
-
-    def events(self):
+    def window(self, h):
+        return pl.ds(pl.multiple_of(h * self.stride + self.offset, 128), self.cols)
+
+    def piece(self, q, h):
+        return self.full.at[pl.ds(pl.multiple_of(q * self.rows, 16), self.rows), self.window(h)]
+
+    def stage(self, kind, r):
         p = self.place
         yes = p.z >= 0
         up = ((p.me + 4, p.core), p.z < ZS - 1)
@@ -392,121 +323,57 @@
         near = ((p.near, p.core), yes)
         far = ((p.far, p.core), yes)
         other = (p.partner(), None)
-        out = [(p.me, yes, [up, down, near, far], True)]
-        for r in range(ZS):
-            ways = [(-4 * r, p.z >= r, up), (4 * r, p.z + r < ZS, down)] if r else [(0, yes, None)]
-            if r:
-                for shift, there, onward in ways:
-                    out.append((p.me + shift, there, [onward, near, far, other], False))
-            for shift, there, _ in ways:
-                out.append((p.near + shift, there, [far, other], False))
-            for shift, there, _ in ways:
-                out.append((p.far + shift, there, [other], False))
-            for shift, there, _ in ways:
-                out.append((p.diag + shift, there, [other], False))
-        return out
-
-    def copies(self, t, event):
-        q, _, targets, _ = event
-        piece = self.piece(t, q, self.place.core)
+        if kind == OWN:
+            return [(p.me, yes, [up, down, near, far])]
+        base = {COLUMN: p.me, NEAR: p.near, FAR: p.far, DIAG: p.diag}[kind]
+        ways = [(-4 * r, p.z >= r, up), (4 * r, p.z + r < ZS, down)] if r else [(0, yes, None)]
+        onward = {COLUMN: [near, far, other], NEAR: [far, other], FAR: [other], DIAG: [other]}[kind]
+        return [(base + shift, there, ([way] if kind == COLUMN else []) + onward) for shift, there, way in ways]
+
+    def copies(self, kind, q, targets):
+        p = self.place
+        dst = self.piece(q, p.core)
+        src = self.own.at[:, self.window(p.core)] if kind == OWN else dst
         made = []
         for n, (dev, cond) in enumerate(targets):
-            recv = self.passed.at[t, q] if cond is None else self.recvs.at[t, q]
-            made.append((send(piece, piece, self.sends.at[t, n, q], recv, dev), cond))
+            recv = self.passed.at[q] if cond is None else self.recvs.at[q]
+            made.append((send(src, dst, self.sends.at[n, q], recv, dev), cond))
         return made
 
-    def run(self, t, event):
-        q, there, targets, own = event
-
-        @pl.when(there)
-        def _():
-            made = self.copies(t, event)
-            if not own:
-                made[0][0].wait_recv() if made[0][1] is not None else send(
-                    self.piece(t, q, self.place.core),
-                    self.piece(t, q, self.place.core),
-                    self.sends.at[t, 0, q],
-                    self.recvs.at[t, q],
-                    self.place.partner(),
-                ).wait_recv()
-            for copy, cond in made:
-                if cond is None:
-                    copy.start()
-                else:
-                    pl.when(cond)(copy.start)
-
-    def finish_sends(self, t, event):
-        q, there, targets, own = event
-
-        @pl.when(there)
-        def _():
-            for copy, cond in self.copies(t, event):
-                if cond is None:
-                    copy.wait_send()
-                else:
-                    pl.when(cond)(copy.wait_send)
-
-    def finish_partner(self, t):
-        p = self.place
-
-        @pl.loop(0, 16)
+    def run(self, kind, r):
+        if kind == END:
+            return self.finish_partner()
+        for q, there, targets in self.stage(kind, r):
+
+            def go(q=q, targets=targets):
+                if kind != OWN:
+                    piece = self.piece(q, self.place.core)
+                    send(piece, piece, self.sends.at[0, q], self.recvs.at[q], self.place.partner()).wait_recv()
+                for copy, cond in self.copies(kind, q, targets):
+                    copy.start() if cond is None else pl.when(cond)(copy.start)
+
+            pl.when(there)(go)
+
+    def finish_sends(self, kind, r):
+        if kind == END:
+            return
+        for q, there, targets in self.stage(kind, r):
+
+            def go(q=q, targets=targets):
+                for copy, cond in self.copies(kind, q, targets):
+                    copy.wait_send() if cond is None else pl.when(cond)(copy.wait_send)
+
+            pl.when(there)(go)
+
+    def finish_partner(self):
+        p = self.place
+
+        @pl.loop(0, 4 * ZS)
         def _(q):
             @pl.when(q != p.me)
             def _():
-                piece = self.piece(t, q, 1 - p.core)
-                send(piece, piece, self.sends.at[t, 0, q], self.passed.at[t, q], p.partner()).wait_recv()
-
-
-def gather_body(count, *refs):
-    shards, fulls = refs[:count], refs[count : 2 * count]
-    own = refs[2 * count : 3 * count]
-    sends, recvs, passed, local = refs[3 * count :]
-    place = Place()
-    sem, expect = place.barrier()
-    for shard, low in zip(shards, own):
-        low[...] = shard[...].astype(low.dtype)
-    rows = [shard.shape[0] for shard in shards]
-    g = Gather(place, fulls, rows, sends, recvs, passed)
-    mine = []
-    for t in range(count):
-        dst = fulls[t].at[pl.ds(pl.multiple_of(place.me * rows[t], 16), rows[t]), :]
-        mine.append(pltpu.make_async_copy(own[t], dst, local.at[t]))
-        mine[t].start()
-    pl.semaphore_wait(sem, expect)
-    events = g.events()
-    for t in range(count):
-        mine[t].wait()
-        g.run(t, events[0])
-    for event in events[1:]:
-        for t in range(count):
-            g.run(t, event)
-    for event in events:
-        for t in range(count):
-            g.finish_sends(t, event)
-    for t in range(count):
-        g.finish_partner(t)
-
-
-def gather_all(shards, dtypes, collective_id):
-    count = len(shards)
-    fulls = [jax.ShapeDtypeStruct((16 * s.shape[0], s.shape[1]), d) for s, d in zip(shards, dtypes)]
-    return pl.pallas_call(
-        functools.partial(gather_body, count),
-        in_specs=[pl.BlockSpec(memory_space=pltpu.VMEM)] * count,
-        out_specs=[pl.BlockSpec(memory_space=pl.ANY)] * count,
-        out_shape=fulls,
-        scratch_shapes=[pltpu.VMEM(s.shape, d) for s, d in zip(shards, dtypes)]
-        + [
-            pltpu.SemaphoreType.DMA((count, 4, 16)),
-            pltpu.SemaphoreType.DMA((count, 16)),
-            pltpu.SemaphoreType.DMA((count, 16)),
-            pltpu.SemaphoreType.DMA((count,)),
-        ],
-        compiler_params=pltpu.CompilerParams(
-            collective_id=collective_id, has_side_effects=True, vmem_limit_bytes=VMEM_LIMIT
-        ),
-        name=f"gather_{collective_id}",
-    )(*shards)
+                piece = self.piece(q, 1 - p.core)
+                send(piece, piece, self.sends.at[0, q], self.passed.at[q], p.partner()).wait_recv()
 
 
 class Scatter:
@@ -528,7 +395,7 @@
         return ref.at[pl.ds(pl.multiple_of(q * self.rows, 16), self.rows), :]
 
     def load(self, ref, q):
-        return ref[pl.ds(pl.multiple_of(q * self.rows, 16), self.rows), :].astype(single)
+        return ref[pl.ds(pl.multiple_of(q * self.rows, 16), self.rows), :]
 
     def store(self, ref, q, value):
         ref[pl.ds(pl.multiple_of(q * self.rows, 16), self.rows), :] = value.astype(ref.dtype)
@@ -674,15 +541,15 @@
 
     def to_last(self):
         p = self.place
-        self.own[...] = self.load(self.near, p.z)
+        self.own[...] = self.load(self.near, p.z).astype(single)
 
         @pl.when(p.z > 0)
         def _():
-            self.own[...] += self.load(self.low, p.z)
+            self.own[...] += self.load(self.low, p.z).astype(single)
 
         @pl.when(p.z < ZS - 1)
         def _():
-            self.own[...] += self.load(self.high, p.z)
+            self.own[...] += self.load(self.high, p.z).astype(single)
 
         self.copy_last().start()
         self.out[:, self.columns(p.core)] = self.own[...]
@@ -806,7 +673,193 @@
 PAIRS = 2
 
 
-def back_body(links, plan, *refs):
+FRONT_PLAN = [
+    (-1, 0, 0, 0), (-1, 1, 0, 0), (-1, 0, 2, 0), (-1, 0, 3, 0), (-1, 0, 1, 1), (-1, 1, 2, 0),
+    (-1, 1, 3, 0), (-1, 1, 1, 1), (-1, 0, 4, 0), (-1, 0, 1, 2), (-1, 1, 1, 2), (-1, 0, 2, 1),
+    (-1, 0, 3, 1), (-1, 1, 4, 0), (-1, 1, 2, 1), (-1, 0, 1, 3), (-1, 0, 2, 2), (-1, 1, 1, 3),
+    (-1, 1, 3, 1), (-1, 1, 2, 2), (-1, 0, 3, 2), (-1, 1, 3, 2), (-1, 0, 2, 3), (-1, 0, 3, 3),
+    (-1, 0, 4, 1), (-1, 1, 2, 3), (-1, 2, 0, 0), (-1, 3, 0, 0), (-1, 4, 0, 0), (-1, 1, 4, 1),
+    (-1, 1, 3, 3), (-1, 0, 4, 2), (-1, 1, 4, 2), (-1, 0, 4, 3), (-1, 1, 4, 3), (-1, 2, 2, 0),
+    (-1, 2, 1, 1), (-1, 0, 5, 0), (-1, 2, 3, 0), (-1, 1, 5, 0), (1, 3, 2, 0), (1, 3, 3, 0),
+    (1, 3, 1, 1), (3, 4, 2, 0), (3, 4, 1, 1), (3, 2, 1, 2), (3, 4, 3, 0), (4, 2, 4, 0),
+    (4, 2, 2, 1), (5, 2, 3, 1), (6, 3, 1, 2), (7, 3, 4, 0), (8, 2, 1, 3), (8, 3, 2, 1),
+    (8, 4, 1, 2), (10, 3, 1, 3), (11, 2, 2, 3), (11, 3, 3, 1), (13, 2, 2, 2), (13, 4, 4, 0),
+    (13, 4, 2, 1), (13, 4, 1, 3), (15, 3, 2, 2), (15, 3, 2, 3), (16, 2, 3, 3), (17, 2, 3, 2),
+    (17, 4, 3, 1), (17, 4, 2, 2), (17, 4, 2, 3), (18, 2, 4, 1), (19, 3, 3, 2), (20, 3, 3, 3),
+    (21, 2, 4, 3), (21, 3, 4, 1), (22, 2, 4, 2), (22, 4, 3, 2), (22, 4, 3, 3), (24, 2, 5, 0),
+    (24, 4, 4, 1), (25, 3, 4, 3), (26, 3, 4, 2), (27, 4, 4, 2), (27, 4, 4, 3), (28, 3, 5, 0),
+    (31, 4, 5, 0),
+]
+SMALL_AT = (0, 8, 14, 23)
+
+
+def front_body(links, *refs):
+    tok_ref, flag_ref, mask_ref, small_ref = refs[:4]
+    step = pl.program_id(0)
+    count = pl.num_programs(0)
+    per_group = 1 + HEADS // (2 * PAIRS)
+    actions = {}
+    if links:
+        shards, (inp_ref, proj_ref, mixed_ref, log_ref, vec_ref) = refs[4:8], refs[8:13]
+        fulls, w_ref, own, rest = refs[13:17], refs[17], refs[18:21], refs[21:]
+        place = Place()
+        local = rest[0]
+        sets = [rest[1 + 3 * n : 4 + 3 * n] for n in range(5)]
+        total = Total(place, small_ref, False, vec_ref, *rest[16:19])
+        rows = [shard.shape[0] for shard in shards]
+        mine = pl.ds(pl.multiple_of(place.me * rows[0], 16), rows[0])
+        cut = w_ref.shape[1] // 2
+        first = cut // 2 // 128 * 128 + 128
+        parts = [
+            Gather(place, w_ref.at[mine], w_ref, rows[0], 0, first, *sets[0]),
+            Gather(place, w_ref.at[mine], w_ref, rows[0], first, cut - first, *sets[1]),
+        ]
+        parts += [Gather(place, own[t], fulls[t + 1], rows[t + 1], 0, fulls[t + 1].shape[1] // 2, *sets[t + 2]) for t in range(3)]
+        keep = pltpu.make_async_copy(w_ref, fulls[0], local.at[0])
+        mine_to = [
+            pltpu.make_async_copy(
+                own[t], fulls[t + 1].at[pl.ds(pl.multiple_of(place.me * rows[t + 1], 16), rows[t + 1]), :], local.at[t + 1]
+            )
+            for t in range(3)
+        ]
+
+        def enter():
+            sem, expect = place.barrier()
+            w_ref[mine, :] = shards[0][...].astype(half)
+            for t in range(3):
+                own[t][...] = shards[t + 1][...].astype(half)
+            pl.semaphore_wait(sem, expect)
+            for copy in mine_to:
+                copy.start()
+
+        stages = total.stages()
+        todo = [(-1, enter), (-1, stages[1])]
+        seen = 0
+        for n, part, kind, r in FRONT_PLAN:
+            if seen in SMALL_AT[1:]:
+                todo.append((-1, stages[1 + SMALL_AT.index(seen)]))
+            todo.append((n, functools.partial(parts[part].run, kind, r)))
+            seen += 1
+        todo.append((0, keep.start))
+
+        def leave():
+            keep.wait()
+            for copy in mine_to:
+                copy.wait()
+            for _, part, kind, r in FRONT_PLAN:
+                parts[part].finish_sends(kind, r)
+
+        for n, action in sorted(todo, key=lambda item: item[0]):
+            actions.setdefault(front_point(per_group, n), []).append(action)
+        actions.setdefault((4 * per_group - 1, 2), []).append(leave)
+    else:
+        w_ref, (inp_ref, proj_ref, mixed_ref, log_ref, vec_ref) = refs[4], refs[5:]
+        vec_ref[...] = small_ref[...]
+
+    def talk(point):
+        for (at, where), todo in sorted(actions.items(), key=lambda item: item[0]):
+            if where == point:
+
+                def run_all(todo=todo):
+                    for action in todo:
+                        action()
+
+                pl.when(step == at)(run_all)
+
+    talk(0)
+    column = step % per_group - 1
+    wide = 128 * PAIRS
+    width = inp_ref.shape[1]
+
+    @pl.when(column < 0)
+    def _():
+        masked = flag_ref[...] > 0
+        low = jnp.where(masked, mask_ref[...].astype(single), tok_ref[...].astype(single)).astype(half)
+        inp_ref[...] = low
+        for n in range(3):
+            cols = pl.ds(n * width, width)
+            value = mm(low, w_ref[:, cols])
+            if n != 1:
+                value = value + vec_ref[pl.ds(n // 2, 1), :]
+            proj_ref[:, cols] = value.astype(half)
+
+    @pl.when(column >= 0)
+    def _():
+        for p in range(PAIRS):
+            start = column * wide + 128 * p
+            q, k, v = (proj_ref[:, pl.ds(pl.multiple_of(start + n * width, 128), 128)] for n in range(3))
+            mixed, logs = attend_pair(q, k, v)
+            mixed_ref[:, pl.ds(128 * p, 128)] = mixed
+            for h in range(2):
+                log_ref[0, 0, pl.ds(2 * p + h, 1), :] = logs[h]
+            if p + 1 < PAIRS:
+                talk(1)
+
+    talk(2)
+
+
+def front_point(per_group, n):
+    points = 1 + (per_group - 1) * PAIRS
+    if n < 0:
+        return (0, 0)
+    if n >= 4 * points:
+        return (4 * per_group - 1, 2)
+    group, n = n // points, n % points
+    if n == 0:
+        return (group * per_group, 0)
+    return (group * per_group + 1 + (n - 1) // PAIRS, (n - 1) % PAIRS)
+
+
+def front(links, tokens, flags, mask_embed, small, shards):
+    count, width = tokens.shape
+    groups = count // SEQ
+    wide = 128 * PAIRS
+    steps = width // wide
+    per_group = steps + 1
+    group = lambda cols: pl.BlockSpec((SEQ, cols), lambda s: (s // per_group, 0))
+    whole = lambda shape: pl.BlockSpec(shape, lambda s: (0,) * len(shape), pipeline_mode=pl.Buffered(1))
+    column = lambda s: jnp.maximum(s % per_group - 1, 0)
+    anywhere = pl.BlockSpec(memory_space=pl.ANY)
+    in_specs = [group(width), group(1), whole((1, width)), whole(small.shape)] + [whole(s.shape) for s in shards]
+    out_specs = [
+        group(width),
+        group(3 * width),
+        pl.BlockSpec((SEQ, wide), lambda s: (s // per_group, column(s))),
+        pl.BlockSpec((1, 1, 8, SEQ), lambda s: (s // per_group, column(s), 0, 0)),
+        whole(small.shape),
+    ]
+    out_shape = [
+        jax.ShapeDtypeStruct((count, width), half),
+        jax.ShapeDtypeStruct((count, 3 * width), half),
+        jax.ShapeDtypeStruct((count, width), half),
+        jax.ShapeDtypeStruct((groups, steps, 8, SEQ), single),
+        jax.ShapeDtypeStruct(small.shape, single),
+    ]
+    scratch = []
+    params = pltpu.CompilerParams(vmem_limit_bytes=VMEM_LIMIT)
+    if links:
+        full = [(4 * ZS * s.shape[0], s.shape[1]) for s in shards]
+        out_specs += [anywhere] * 4
+        out_shape += [jax.ShapeDtypeStruct(shape, half) for shape in full]
+        scratch += [pltpu.VMEM(full[0], half)] + [pltpu.VMEM(s.shape, half) for s in shards[1:]]
+        scratch.append(pltpu.SemaphoreType.DMA((4,)))
+        for _ in range(5):
+            scratch += [pltpu.SemaphoreType.DMA((4, 4 * ZS))] + [pltpu.SemaphoreType.DMA((4 * ZS,))] * 2
+        scratch += Total.scratch(small.shape)
+        params = pltpu.CompilerParams(collective_id=1, has_side_effects=True, vmem_limit_bytes=VMEM_LIMIT)
+    return pl.pallas_call(
+        functools.partial(front_body, links),
+        grid=(groups * per_group,),
+        in_specs=in_specs,
+        out_specs=out_specs,
+        out_shape=out_shape,
+        scratch_shapes=scratch,
+        compiler_params=params,
+        name="front",
+    )(tokens, flags, mask_embed, small, *shards)
+
+
+def back_body(links, steps, *refs):
     q_ref, k_ref, v_ref, grad_ref, mixed_ref, log_ref, inp_ref, w_ref, dsum_ref, flag_ref, small_ref = refs[:11]
     rest = refs[11:]
     step = pl.program_id(0)
@@ -833,10 +886,10 @@
             sem, expect = place.barrier()
             pl.semaphore_wait(sem, expect)
 
-        actions.setdefault((0, 0), []).append(enter)
-        for n, run in enumerate(runs):
-            for stage, when in zip(run.stages(), plan[n]):
-                actions.setdefault(when, []).append(stage)
+        actions[(0, 0)] = [enter]
+        order = [(n, which, stage) for which, row in enumerate(BACK_PLAN) for stage, n in enumerate(row)]
+        for n, which, stage in sorted(order):
+            actions.setdefault(back_point(attends, steps, n), []).append(runs[which].stages()[stage])
     else:
         out_ref, made, total_ref = rest[:3]
         parts_ref, sums = rest[3:]
@@ -917,6 +970,7 @@
     attends = groups * per_group
     weights = 3 * (width // 256)
     block = 256
+    steps = attends + weights + count // block
     last = attends - 1
 
     def group_of(s):
@@ -949,7 +1003,6 @@
     operands = [projected, projected, projected, d_mixed, mixed, logs, inputs, w_qkv, d_sum, flags, small]
     dparts = pltpu.VMEM((3, count, width), half)
     sums = pltpu.VMEM(small.shape, single)
-    plan = None
     if links:
         in_specs += [anywhere] * 3
         operands += grads
@@ -961,15 +1014,14 @@
             scratch += Scatter.scratch(shape)
         scratch += Total.scratch(small.shape)
         params = pltpu.CompilerParams(collective_id=2, has_side_effects=True, vmem_limit_bytes=VMEM_LIMIT)
-        plan = back_plan(attends, weights, count // block)
     else:
         out_specs += [whole((3, width, width)), whole(small.shape)]
         out_shape += [jax.ShapeDtypeStruct((3, width, width), half), jax.ShapeDtypeStruct(small.shape, single)]
         scratch = [dparts, sums]
         params = pltpu.CompilerParams(vmem_limit_bytes=VMEM_LIMIT)
     return pl.pallas_call(
-        functools.partial(back_body, links, plan),
-        grid=(attends + weights + count // block,),
+        functools.partial(back_body, links, steps),
+        grid=(steps,),
         in_specs=in_specs,
         out_specs=out_specs,
         out_shape=out_shape,
@@ -979,63 +1031,54 @@
     )(*operands)
 
 
-def back_plan(attends, weights, inputs):
-    def at(n):
-        if n < 2 * attends:
-            return n // 2, n % 2
-        n -= 2 * attends
-        return (attends + n, 0) if n < weights + inputs else (attends + weights + inputs - 1, 2)
-
-    down = [0, 3, 11, 18, 20, 22, 23, 24, 25]
-    up = [0, 5, 19, 25, 27, 28, 29, 30, 31]
-    out = [0, 6, 21, 26, 28, 29, 30, 31, 32]
-    third = lambda n: [n, n + 1, n + 4, n + 6, n + 8, n + 9, n + 10, n + 11, 99]
-    small = [33, 34, 36, 38, 40]
-    after = 2 * attends
-    table = [down, up, out, third(after + 3), third(after + 6), third(after + 9), small]
-    return [[at(n) for n in row] for row in table]
-
-
-def pack_small(vectors, b_up, low):
-    n = vectors[0].shape[0]
-    block = jnp.concatenate([jnp.stack(vectors), b_up.reshape(-1, n)])
-    block = lax.reduce_precision(block, 8, 7) if low else block
-    return jnp.pad(block, ((0, 16 - block.shape[0]), (0, 128 - n)))
-
-
-def unpack_small(full, chips, n):
-    full = full.reshape(chips, 16, 128)
-    vectors = full[:, :8, :n].transpose(1, 0, 2).reshape(8, chips * n)
-    return vectors, full[:, 8:12, :n].reshape(1, 4 * chips * n)
+BACK_PLAN = [
+    [0, 4, 13, 22, 29, 34, 36, 36, 37],
+    [0, 6, 23, 28, 34, 38, 41, 41, 45],
+    [0, 6, 24, 29, 35, 38, 41, 41, 45],
+    [27, 29, 33, 35, 37, 39, 41, 41, 45],
+    [30, 32, 35, 37, 39, 41, 50, 50, 55],
+    [33, 34, 37, 39, 41, 52, 62, 62, 67],
+    [33, 35, 37, 39, 42],
+]
+
+
+def back_point(attends, steps, n):
+    if n < 2 * attends:
+        return n // 2, n % 2
+    n -= attends
+    return (n, 0) if n < steps else (steps - 1, 2)
 
 
 def local(chips, twins, tokens, flags, mask_embed, cotangent, w_qkv, b_qv, w_out, b_out, norm_one, w_up, b_up, w_down, b_down, norm_two):
-    own_kernels = chips == 16 and twins == 2
+    links = chips == 4 * ZS and twins == 2
     n = b_out.shape[0]
     width = chips * n
-    small = pack_small(
-        [b_qv[0], b_qv[1], b_out, norm_one[0], norm_one[1], b_down, norm_two[0], norm_two[1]], b_up, True
-    )
+    me = lax.axis_index("dp")
+    vectors = jnp.stack([b_qv[0], b_qv[1], b_out, norm_one[0], norm_one[1], b_down, norm_two[0], norm_two[1]])
+    vectors = lax.dynamic_update_slice(jnp.zeros((8, width), single), vectors, (0, me * n))
+    hidden = lax.dynamic_update_slice(jnp.zeros((4 * width,), single), b_up, (me * 4 * n,)).reshape(4, width)
+    small = jnp.concatenate([vectors, hidden, jnp.zeros_like(hidden)])
+    small = lax.reduce_precision(small, 8, 7)
     shards = [w_qkv, w_out, w_up, w_down]
-    if own_kernels:
-        *fulls, small_full = gather_all(shards + [small], [half] * 4 + [single], 1)
+    flag_col = flags[:, None]
+    if links:
+        inputs, projected, mixed, logs, vecs, qkv_full, out_full, up_full, down_full = front(
+            True, tokens, flag_col, mask_embed[None], small, shards
+        )
     else:
-        fulls = [lax.all_gather(s.astype(half), "dp", axis=0, tiled=True) for s in shards]
-        small_full = lax.all_gather(small, "dp", axis=0, tiled=True)
-    qkv_full, out_full, up_full, down_full = fulls
-    vecs, bup_full = unpack_small(small_full, chips, n)
-    bias = jnp.concatenate([vecs[0], jnp.zeros_like(vecs[0]), vecs[1]])[None]
-    flag_col = flags[:, None]
-    inputs, projected = project(tokens, flag_col, mask_embed[None], qkv_full, bias)
-    mixed, logs = attend(projected)
+        qkv_full, out_full, up_full, down_full = [
+            lax.all_gather(s.astype(half), "dp", axis=0, tiled=True) for s in shards
+        ]
+        small = lax.psum(small, "dp")
+        inputs, projected, mixed, logs, vecs = front(False, tokens, flag_col, mask_embed[None], small, [qkv_full])
     activations, d_sum, d_mixed, g_small, g_out, g_up, g_down = middle(
-        mixed, inputs, flag_col, cotangent, vecs, bup_full, out_full, up_full, down_full
+        mixed, inputs, flag_col, cotangent, vecs, out_full, up_full, down_full
     )
     grads = [g_out, g_up, g_down]
     input_grad, g_qkv, *summed = back(
-        own_kernels, projected, d_mixed, mixed, logs, inputs, qkv_full, d_sum, flag_col, g_small, grads
+        links, projected, d_mixed, mixed, logs, inputs, qkv_full, d_sum, flag_col, g_small, grads
     )
-    if own_kernels:
+    if links:
         g_out, g_up, g_down, g_small = summed
     else:
         g_small = summed[0]
@@ -1043,7 +1086,6 @@
         grads = [lax.psum_scatter(g.astype(single), "dp", scatter_dimension=0, tiled=True) for g in grads]
         g_qkv, g_out, g_up, g_down = [lax.psum(g.astype(half), "rep").astype(single) for g in grads]
         g_small = lax.psum(g_small, ("dp", "rep"))
-    me = lax.axis_index("dp")
     rows = lax.dynamic_slice_in_dim(g_small[:8], me * n, n, axis=1)
     g_bup = lax.dynamic_slice_in_dim(g_small[8:12].reshape(4 * width), me * 4 * n, 4 * n)
     return (

time: 380 us -> 314 us (0.83)
  Pallas kernels: 357 us -> 295 us
  local copies, waits for them, and re-layouts: 21.8 us -> 17.7 us
    pallas_call x4 -> x2, Pallas kernels: 249 us -> 187 us  [the longest x1 103 us: back(): pl.pallas_call(functools.partial(back_body, links, steps), grid=(steps,),...]
where the time goes in v3:
time: 314 us
  Pallas kernels  295 us (94%)
  local copies, waits for them, and re-layouts  17.7 us (6%)
    pallas_call x1, Pallas kernels, middle(): pl.pallas_call(middle_body, grid=(count // block,), in_specs=[rows(width)...  108 us
    pallas_call x1, Pallas kernels, back(): pl.pallas_call(functools.partial(back_body, links, steps), grid=(steps,),...  103 us
    pallas_call x1, Pallas kernels, front(): pl.pallas_call(functools.partial(front_body, links), grid=(groups * per_g...  83.9 us
    unnamed x13, local copies, waits for them, and re-layouts  9.09 us

profile of v3, /device:TPU:0, one launch (start us, length us, event | category | flops | bytes accessed | tf_op | source)
XLA Modules:
  0.0 313.6 jit_solution(17118033731098170733)
XLA Ops:
  0.7 0.1 pad.2.clone
  0.7 1.3 broadcast_in_dim.16.refs_2_
  2.0 0.8 stack.12
  2.8 0.9 dynamic_update_slice.7
  3.7 0.3 dynamic_update_slice.6
  3.9 0.7 maximum_reduce-precision_fusion.refs_3_
  4.6 2.0 copy.26.refs_1_.flag_ref.refs_9_
  6.7 83.9 %front.1 = (bf16[2048,768]{1,0:T(8,128)(2,1)}, bf16[2048,2304]{1,0:T(8,128)(2,1)}, bf16[2048,768]{1,0:T(8,128)(2,1)}, f32[4,3,8,512]{3,2,1,0:T(8,128)}, f32[16,7...) custom-call(bf16[2048,768]{1,0:T(8,128)(2,1)} %refs_0_.1, ...), custom_call_target="tpu_custom_call" | custom-call | tf_op jit(solution)/shard_map/front/pallas_call | solution.py:850
  90.5 108.0 %middle.1 = (bf16[2048,768]{1,0:T(8,128)(2,1)}, f32[2048,768]{1,0:T(8,128)}, bf16[2048,768]{1,0:T(8,128)(2,1)}, f32[16,768]{1,0:T(8,128)}, bf16[768,768]{1,0:T(8...) custom-call(bf16[2048,768]{1,0:T(8,128)(2,1)} %get-tuple-element.34.mixed_ref.refs_4_, ...), custom_call_target="tpu_custom_call" | custom-call | tf_op jit(solution)/shard_map/middle/pallas_call | solution.py:209
  198.6 102.7 %back.1 = (f32[2048,768]{1,0:T(8,128)}, f32[48,2304]{1,0:T(8,128)}, f32[48,768]{1,0:T(8,128)}, f32[48,3072]{1,0:T(8,128)}, f32[192,768]{1,0:T(8,128)}, /*index=5*/f32[16,768]{1,0:T(8,128)}) custom-call(bf16[2048,2304]{1,0:T(8,128)(2,1)} %get-tuple-element.41.refs_0_.refs_1_.refs_2_, bf16[2048,2304]{1,0:T(8,128)(2,1)} %get-tuple-element.41.refs_0_.refs_1_.refs_2_, ...), custom_call_target="tpu_custom_call" | custom-call | tf_op jit(solution)/shard_map/back/pallas_call | solution.py:1022
  301.2 0.7 slice.34
  302.0 0.7 slice.30
  302.7 0.1 constant_dynamic-slice_fusion
  302.8 0.6 dynamic_slice.7
  303.4 0.5 slice_bitcast_fusion
  303.9 0.6 fusion
  304.5 6.0 %copy.36 = f32[2048,768]{1,0:T(8,128)} copy(f32[2048,768]{1,0:T(8,128)} %get-tuple-element.74) | data formatting | bytes 12582912
  310.5 0.0 copy-done.2
  310.5 0.8 copy.37
  311.3 0.0 copy-done.3
  311.3 0.7 copy.38
  312.0 0.0 copy-done.1
  312.0 0.8 copy.39
  312.8 0.8 copy.40
  (10 shorter events, 0.0 us)
Async XLA Ops:
  304.5 6.0 %copy-start.2 = (f32[48,2304]{1,0:T(8,128)S(1)}, f32[48,2304]{1,0:T(8,128)}, u32[]{:S(2)}) copy-start(f32[48,2304]{1,0:T(8,128)} %get-tuple-element.75) | copy-start | bytes 1327108
  304.5 6.8 %copy-start.3 = (f32[48,768]{1,0:T(8,128)S(1)}, f32[48,768]{1,0:T(8,128)}, u32[]{:S(2)}) copy-start(f32[48,768]{1,0:T(8,128)} %get-tuple-element.77) | copy-start | bytes 442372
  304.5 7.5 %copy-start.1 = (f32[48,3072]{1,0:T(8,128)S(1)}, f32[48,3072]{1,0:T(8,128)}, u32[]{:S(2)}) copy-start(f32[48,3072]{1,0:T(8,128)} %get-tuple-element.80) | copy-start | bytes 1769476
  304.5 8.3 %copy-start = (f32[192,768]{1,0:T(8,128)S(1)}, f32[192,768]{1,0:T(8,128)}, u32[]{:S(2)}) copy-start(f32[192,768]{1,0:T(8,128)} %get-tuple-element.82) | copy-start | bytes 1769476

commit v4 on v3

--- a/solution.py
+++ b/solution.py
@@ -96,9 +96,9 @@
     flag_ref,
     cot_ref,
     vec_ref,
-    wo_ref,
-    wu_ref,
-    wd_ref,
+    wo_all,
+    wu_all,
+    wd_all,
     act_out,
     dsum_out,
     dmix_out,
@@ -106,59 +106,86 @@
     gwo_out,
     gwu_out,
     gwd_out,
+    wo_ref,
+    wu_ref,
+    wd_ref,
     unit1,
-    first,
+    scale1,
     low,
+    upper_ref,
     acts,
     slope,
-    total,
     d_low,
     acc_o,
     acc_u,
     acc_d,
     stage,
     sems,
+    loads,
 ):
     step = pl.program_id(0)
     last = pl.num_programs(0) - 1
     width = wo_ref.shape[0]
     chunks = wd_ref.shape[0] // width
+    block = low.shape[0]
+    total = dsum_out
+    parts = [pl.ds(n * (block // SPLIT), block // SPLIT) for n in range(SPLIT)]
 
     @pl.when(step == 0)
     def _():
+        weights = [(wo_all, wo_ref), (wu_all, wu_ref), (wd_all, wd_ref)]
+        copies = [pltpu.make_async_copy(src, dst, loads.at[n]) for n, (src, dst) in enumerate(weights)]
+        for copy in copies:
+            copy.start()
         small_out[...] = jnp.zeros_like(small_out)
         acc_o[...] = jnp.zeros_like(acc_o)
         acc_u[...] = jnp.zeros_like(acc_u)
         acc_d[...] = jnp.zeros_like(acc_d)
+        for copy in copies:
+            copy.wait()
 
     vec = lambda row: vec_ref[pl.ds(row, 1), :]
-    attended = mm(mixed_ref[...], wo_ref[...]) + vec(2)
-    value, unit, inv1 = norm(inp_ref[...].astype(single) + attended, vec(3), vec(4))
-    unit1[...] = unit
-    first[...] = value
-    low[...] = value.astype(half)
-    total[...] = jnp.zeros_like(total)
-
-    @pl.loop(0, chunks)
-    def _(j):
+    for rows in parts:
+        attended = mm(mixed_ref[rows, :], wo_ref[...]) + vec(2)
+        value, unit, inverse = norm(inp_ref[rows, :].astype(single) + attended, vec(3), vec(4))
+        unit1[rows, :] = unit
+        scale1[rows, :] = inverse
+        total[rows, :] = value + vec(5)
+        low[rows, :] = value.astype(half)
+
+    def to_upper(j):
+        upper_ref[j % 2] = mm(low[...], wu_ref[:, j * width : (j + 1) * width]) + vec(8 + j)
+
+    to_upper(0)
+    for j in range(chunks):
+        if j + 1 < chunks:
+            to_upper(j + 1)
+        upper = upper_ref[j % 2]
+        scaled = upper * 0.7071067811865476
+        phi = 0.5 * (1.0 + lax.erf(scaled))
+        acts[j] = (upper * phi).astype(half)
+        bell = jnp.exp2(scaled * scaled * -1.4426950408889634)
+        slope[j] = (phi + upper * bell * 0.3989422804014327).astype(half)
+        total[...] += mm(acts[j], wd_ref[j * width : (j + 1) * width, :])
+
+    for rows in parts:
+        value, unit, inv2 = norm(total[rows, :], vec(6), vec(7))
+        act_out[rows, :] = value.astype(half)
+        out_grad = jnp.where(flag_ref[rows, :] > 0, cot_ref[rows, :].astype(single), 0.0)
+        small_out[pl.ds(6, 1), :] += col_sum(out_grad * unit)
+        small_out[pl.ds(7, 1), :] += col_sum(out_grad)
+        d_second = norm_back(out_grad, unit, inv2, vec(6))
+        lowered = d_second.astype(half)
+        d_low[rows, :] = lowered
+        small_out[pl.ds(5, 1), :] += col_sum(lowered.astype(single))
+        total[rows, :] = d_second
+
+    def copy_out(j):
         cols = pl.ds(pl.multiple_of(j * width, width), width)
-        upper = mm(low[...], wu_ref[:, cols]) + vec(8 + j)
-        phi = 0.5 * (1.0 + lax.erf(upper * 0.7071067811865476))
-        act = (upper * phi).astype(half)
-        acts[j] = act
-        slope[j] = (phi + upper * jnp.exp(-0.5 * upper * upper) * 0.3989422804014327).astype(half)
-        total[...] += mm(act, wd_ref[cols, :])
-
-    value, unit, inv2 = norm(first[...] + total[...] + vec(5), vec(6), vec(7))
-    act_out[...] = value.astype(half)
-    out_grad = jnp.where(flag_ref[...] > 0, cot_ref[...].astype(single), 0.0)
-    small_out[pl.ds(6, 1), :] += col_sum(out_grad * unit)
-    small_out[pl.ds(7, 1), :] += col_sum(out_grad)
-    d_second = norm_back(out_grad, unit, inv2, vec(6))
-    lowered = d_second.astype(half)
-    d_low[...] = lowered
-    small_out[pl.ds(5, 1), :] += col_sum(lowered.astype(single))
-    total[...] = d_second
+        return [
+            pltpu.make_async_copy(stage.at[0], gwd_out.at[cols, :], sems.at[0]),
+            pltpu.make_async_copy(stage.at[1], gwu_out.at[:, cols], sems.at[1]),
+        ]
 
     @pl.loop(0, chunks)
     def _(j):
@@ -170,32 +197,39 @@
         acc_d[j] += mm_ta(acts[j], d_low[...])
         acc_u[j] += mm_ta(low[...], d_upper)
 
+        @pl.when(step == last)
+        def _():
+            @pl.when(j > 0)
+            def _():
+                for copy in copy_out(j - 1):
+                    copy.wait()
+
+            for n, acc in enumerate((acc_d, acc_u)):
+                stage[n] = acc[j].astype(half)
+                copy_out(j)[n].start()
+
     d_first = total[...]
     unit = unit1[...]
     small_out[pl.ds(3, 1), :] += col_sum(d_first * unit)
     small_out[pl.ds(4, 1), :] += col_sum(d_first)
-    d_sum = norm_back(d_first, unit, inv1, vec(3))
+    d_sum = norm_back(d_first, unit, scale1[...], vec(3))
     dsum_out[...] = d_sum
-    d_att = d_sum.astype(half)
-    small_out[pl.ds(2, 1), :] += col_sum(d_att.astype(single))
-    dmix_out[...] = mm_tb(d_att, wo_ref[...]).astype(half)
-    acc_o[...] += mm_ta(mixed_ref[...], d_att)
+    d_low[...] = d_sum.astype(half)
+    small_out[pl.ds(2, 1), :] += col_sum(d_low[...].astype(single))
+    dmix_out[...] = mm_tb(d_low[...], wo_ref[...]).astype(half)
+    acc_o[...] += mm_ta(mixed_ref[...], d_low[...])
 
     @pl.when(step == last)
     def _():
-        copies = []
-        todo = [(acc_d.at[j], gwd_out.at[pl.ds(j * width, width), :]) for j in range(chunks)]
-        todo += [(acc_u.at[j], gwu_out.at[:, pl.ds(j * width, width)]) for j in range(chunks)]
-        todo += [(acc_o, gwo_out)]
-        for n, (src, dst) in enumerate(todo):
-            slot = n % 2
-            if n >= 2:
-                copies[n - 2].wait()
-            stage[slot] = src[...].astype(half)
-            copies.append(pltpu.make_async_copy(stage.at[slot], dst, sems.at[slot]))
-            copies[n].start()
-        for copy in copies[-2:]:
+        for copy in copy_out(chunks - 1):
             copy.wait()
+        stage[0] = acc_o[...].astype(half)
+        copy = pltpu.make_async_copy(stage.at[0], gwo_out, sems.at[0])
+        copy.start()
+        copy.wait()
+
+
+SPLIT = 2
 
 
 def middle(mixed, inputs, flags, cotangent, vecs, w_out, w_up, w_down, block=512):
@@ -203,7 +237,6 @@
     hidden = w_up.shape[1]
     chunks = hidden // width
     rows = lambda cols: pl.BlockSpec((block, cols), lambda i: (i, 0))
-    once = lambda shape: pl.BlockSpec(shape, lambda i: (0, 0), pipeline_mode=pl.Buffered(1))
     keep = lambda shape: pl.BlockSpec(shape, lambda i: (0, 0))
     whole = pl.BlockSpec(memory_space=pl.ANY)
     return pl.pallas_call(
@@ -215,9 +248,9 @@
             rows(1),
             rows(width),
             keep((16, width)),
-            once((width, width)),
-            once((width, hidden)),
-            once((hidden, width)),
+            whole,
+            whole,
+            whole,
         ],
         out_specs=[
             rows(width),
@@ -238,18 +271,22 @@
             jax.ShapeDtypeStruct((hidden, width), half),
         ],
         scratch_shapes=[
+            pltpu.VMEM((width, width), half),
+            pltpu.VMEM((width, hidden), half),
+            pltpu.VMEM((hidden, width), half),
             pltpu.VMEM((block, width), single),
-            pltpu.VMEM((block, width), single),
+            pltpu.VMEM((block, 1), single),
             pltpu.VMEM((block, width), half),
+            pltpu.VMEM((2, block, width), single),
             pltpu.VMEM((chunks, block, width), half),
             pltpu.VMEM((chunks, block, width), half),
-            pltpu.VMEM((block, width), single),
             pltpu.VMEM((block, width), half),
             pltpu.VMEM((width, width), single),
             pltpu.VMEM((chunks, width, width), single),
             pltpu.VMEM((chunks, width, width), single),
             pltpu.VMEM((2, width, width), half),
             pltpu.SemaphoreType.DMA((2,)),
+            pltpu.SemaphoreType.DMA((3,)),
         ],
         compiler_params=pltpu.CompilerParams(vmem_limit_bytes=VMEM_LIMIT),
         name="middle",

time: 314 us -> 302 us (0.962)
  Pallas kernels: 295 us -> 283 us
    pallas_call x1, Pallas kernels: 108 us -> 96.3 us  [middle(): pl.pallas_call(middle_body, grid=(count // block,), in_specs=[rows(width)...]
where the time goes in v4:
time: 302 us
  Pallas kernels  283 us (94%)
  local copies, waits for them, and re-layouts  17.7 us (6%)
    pallas_call x1, Pallas kernels, back(): pl.pallas_call(functools.partial(back_body, links, steps), grid=(steps,),...  102 us
    pallas_call x1, Pallas kernels, middle(): pl.pallas_call(middle_body, grid=(count // block,), in_specs=[rows(width)...  96.3 us
    pallas_call x1, Pallas kernels, front(): pl.pallas_call(functools.partial(front_body, links), grid=(groups * per_g...  83.9 us
    unnamed x13, local copies, waits for them, and re-layouts  9.09 us

profile of v4, /device:TPU:0, one launch (start us, length us, event | category | flops | bytes accessed | tf_op | source)
XLA Modules:
  0.0 301.6 jit_solution(5871198487875996191)
XLA Ops:
  0.7 0.1 pad.2.clone
  0.7 1.3 broadcast_in_dim.16.refs_2_
  2.0 0.8 stack.12
  2.8 0.9 dynamic_update_slice.7
  3.7 0.3 dynamic_update_slice.6
  3.9 0.7 maximum_reduce-precision_fusion.refs_3_
  4.6 2.0 copy.26.refs_1_.flag_ref.refs_9_
  6.7 83.9 %front.1 = (bf16[2048,768]{1,0:T(8,128)(2,1)}, bf16[2048,2304]{1,0:T(8,128)(2,1)}, bf16[2048,768]{1,0:T(8,128)(2,1)}, f32[4,3,8,512]{3,2,1,0:T(8,128)}, f32[16,7...) custom-call(bf16[2048,768]{1,0:T(8,128)(2,1)} %refs_0_.1, ...), custom_call_target="tpu_custom_call" | custom-call | tf_op jit(solution)/shard_map/front/pallas_call | solution.py:887
  90.5 96.3 %middle.1 = (bf16[2048,768]{1,0:T(8,128)(2,1)}, f32[2048,768]{1,0:T(8,128)}, bf16[2048,768]{1,0:T(8,128)(2,1)}, f32[16,768]{1,0:T(8,128)}, bf16[768,768]{1,0:T(8...) custom-call(bf16[2048,768]{1,0:T(8,128)(2,1)} %get-tuple-element.34.mixed_ref.refs_4_, ...), custom_call_target="tpu_custom_call" | custom-call | tf_op jit(solution)/shard_map/middle/pallas_call | solution.py:242
  186.8 102.4 %back.1 = (f32[2048,768]{1,0:T(8,128)}, f32[48,2304]{1,0:T(8,128)}, f32[48,768]{1,0:T(8,128)}, f32[48,3072]{1,0:T(8,128)}, f32[192,768]{1,0:T(8,128)}, /*index=5*/f32[16,768]{1,0:T(8,128)}) custom-call(bf16[2048,2304]{1,0:T(8,128)(2,1)} %get-tuple-element.41.refs_0_.refs_1_.refs_2_, bf16[2048,2304]{1,0:T(8,128)(2,1)} %get-tuple-element.41.refs_0_.refs_1_.refs_2_, ...), custom_call_target="tpu_custom_call" | custom-call | tf_op jit(solution)/shard_map/back/pallas_call | solution.py:1059
  289.3 0.7 slice.34
  290.0 0.7 slice.30
  290.7 0.1 constant_dynamic-slice_fusion
  290.8 0.6 dynamic_slice.7
  291.5 0.5 slice_bitcast_fusion
  292.0 0.6 fusion
  292.6 6.0 %copy.36 = f32[2048,768]{1,0:T(8,128)} copy(f32[2048,768]{1,0:T(8,128)} %get-tuple-element.74) | data formatting | bytes 12582912
  298.6 0.0 copy-done.2
  298.6 0.8 copy.37
  299.3 0.0 copy-done.3
  299.3 0.7 copy.38
  300.0 0.0 copy-done.1
  300.0 0.8 copy.39
  300.8 0.8 copy.40
  (10 shorter events, 0.0 us)
Async XLA Ops:
  292.5 6.0 %copy-start.2 = (f32[48,2304]{1,0:T(8,128)S(1)}, f32[48,2304]{1,0:T(8,128)}, u32[]{:S(2)}) copy-start(f32[48,2304]{1,0:T(8,128)} %get-tuple-element.75) | copy-start | bytes 1327108
  292.6 6.8 %copy-start.3 = (f32[48,768]{1,0:T(8,128)S(1)}, f32[48,768]{1,0:T(8,128)}, u32[]{:S(2)}) copy-start(f32[48,768]{1,0:T(8,128)} %get-tuple-element.77) | copy-start | bytes 442372
  292.6 7.5 %copy-start.1 = (f32[48,3072]{1,0:T(8,128)S(1)}, f32[48,3072]{1,0:T(8,128)}, u32[]{:S(2)}) copy-start(f32[48,3072]{1,0:T(8,128)} %get-tuple-element.80) | copy-start | bytes 1769476
  292.6 8.3 %copy-start = (f32[192,768]{1,0:T(8,128)S(1)}, f32[192,768]{1,0:T(8,128)}, u32[]{:S(2)}) copy-start(f32[192,768]{1,0:T(8,128)} %get-tuple-element.82) | copy-start | bytes 1769476

commit v5 on v4

--- a/solution.py
+++ b/solution.py
@@ -715,9 +715,9 @@
     (-1, 1, 3, 0), (-1, 1, 1, 1), (-1, 0, 4, 0), (-1, 0, 1, 2), (-1, 1, 1, 2), (-1, 0, 2, 1),
     (-1, 0, 3, 1), (-1, 1, 4, 0), (-1, 1, 2, 1), (-1, 0, 1, 3), (-1, 0, 2, 2), (-1, 1, 1, 3),
     (-1, 1, 3, 1), (-1, 1, 2, 2), (-1, 0, 3, 2), (-1, 1, 3, 2), (-1, 0, 2, 3), (-1, 0, 3, 3),
-    (-1, 0, 4, 1), (-1, 1, 2, 3), (-1, 2, 0, 0), (-1, 3, 0, 0), (-1, 4, 0, 0), (-1, 1, 4, 1),
-    (-1, 1, 3, 3), (-1, 0, 4, 2), (-1, 1, 4, 2), (-1, 0, 4, 3), (-1, 1, 4, 3), (-1, 2, 2, 0),
-    (-1, 2, 1, 1), (-1, 0, 5, 0), (-1, 2, 3, 0), (-1, 1, 5, 0), (1, 3, 2, 0), (1, 3, 3, 0),
+    (-1, 0, 4, 1), (-1, 1, 2, 3), (-1, 1, 4, 1), (-1, 1, 3, 3), (-1, 0, 4, 2), (-1, 1, 4, 2),
+    (-1, 0, 4, 3), (-1, 1, 4, 3), (-1, 0, 5, 0), (-1, 1, 5, 0), (0, 2, 0, 0), (0, 3, 0, 0),
+    (0, 4, 0, 0), (0, 2, 2, 0), (0, 2, 1, 1), (0, 2, 3, 0), (1, 3, 2, 0), (1, 3, 3, 0),
     (1, 3, 1, 1), (3, 4, 2, 0), (3, 4, 1, 1), (3, 2, 1, 2), (3, 4, 3, 0), (4, 2, 4, 0),
     (4, 2, 2, 1), (5, 2, 3, 1), (6, 3, 1, 2), (7, 3, 4, 0), (8, 2, 1, 3), (8, 3, 2, 1),
     (8, 4, 1, 2), (10, 3, 1, 3), (11, 2, 2, 3), (11, 3, 3, 1), (13, 2, 2, 2), (13, 4, 4, 0),
@@ -727,7 +727,7 @@
     (24, 4, 4, 1), (25, 3, 4, 3), (26, 3, 4, 2), (27, 4, 4, 2), (27, 4, 4, 3), (28, 3, 5, 0),
     (31, 4, 5, 0),
 ]
-SMALL_AT = (0, 8, 14, 23)
+SMALL_AT = (2, 20, 27, 32)
 
 
 def front_body(links, *refs):
@@ -770,10 +770,10 @@
                 copy.start()
 
         stages = total.stages()
-        todo = [(-1, enter), (-1, stages[1])]
+        todo = [(-1, enter)]
         seen = 0
         for n, part, kind, r in FRONT_PLAN:
-            if seen in SMALL_AT[1:]:
+            if seen in SMALL_AT:
                 todo.append((-1, stages[1 + SMALL_AT.index(seen)]))
             todo.append((n, functools.partial(parts[part].run, kind, r)))
             seen += 1
@@ -992,7 +992,7 @@
         grad = dsum_ref[...]
         for n in range(3):
             grad = grad + mm_tb(parts_ref[n, rows, :], w_ref[:, pl.ds(n * width, width)])
-        out_ref[...] = jnp.where(flag_ref[...] > 0, 0.0, grad)
+        out_ref[...] = jnp.where(flag_ref[...] > 0, 0.0, grad).astype(half)
 
     talk(2)
     if not links:
@@ -1036,7 +1036,7 @@
         whole(small.shape),
     ]
     out_specs = [pl.BlockSpec((block, width), lambda s: (late(s), 0))]
-    out_shape = [jax.ShapeDtypeStruct((count, width), single)]
+    out_shape = [jax.ShapeDtypeStruct((count, width), half)]
     operands = [projected, projected, projected, d_mixed, mixed, logs, inputs, w_qkv, d_sum, flags, small]
     dparts = pltpu.VMEM((3, count, width), half)
     sums = pltpu.VMEM(small.shape, single)
@@ -1127,7 +1127,7 @@
     g_bup = lax.dynamic_slice_in_dim(g_small[8:12].reshape(4 * width), me * 4 * n, 4 * n)
     return (
         activations,
-        input_grad,
+        input_grad.astype(single),
         g_qkv,
         rows[0:2],
         g_out,

time: 302 us -> 302 us (level)
  local copies, waits for them, and re-layouts: 17.7 us -> 11.6 us
  other arithmetic: 0.7 us -> 5.9 us
    unnamed x13 -> x12, local copies, waits for them, and re-layouts: 9.09 us -> 3.07 us
    convert_element_type x0 -> x1, other arithmetic: none -> 5.21 us  [local(): input_grad.astype(single)]
where the time goes in v5:
time: 302 us; the launch traced here: 301 us
  Pallas kernels  283 us (94%)
  local copies, waits for them, and re-layouts  11.6 us (4%)
  other arithmetic  5.9 us (2%)
    pallas_call x1, Pallas kernels, back(): pl.pallas_call(functools.partial(back_body, links, steps), grid=(steps,),...  101 us
    pallas_call x1, Pallas kernels, middle(): pl.pallas_call(middle_body, grid=(count // block,), in_specs=[rows(width)...  96.3 us
    pallas_call x1, Pallas kernels, front(): pl.pallas_call(functools.partial(front_body, links), grid=(groups * per_g...  85.3 us

profile of v5, /device:TPU:0, one launch (start us, length us, event | category | flops | bytes accessed | tf_op | source)
XLA Modules:
  0.0 301.3 jit_solution(3514835501677365322)
XLA Ops:
  0.7 0.1 pad.2.clone
  0.7 1.3 broadcast_in_dim.16.refs_2_
  2.0 0.8 stack.12
  2.8 0.9 dynamic_update_slice.7
  3.7 0.3 dynamic_update_slice.6
  3.9 0.7 maximum_reduce-precision_fusion.refs_3_
  4.6 2.0 copy.26.refs_1_.flag_ref.refs_9_
  6.7 85.3 %front.1 = (bf16[2048,768]{1,0:T(8,128)(2,1)}, bf16[2048,2304]{1,0:T(8,128)(2,1)}, bf16[2048,768]{1,0:T(8,128)(2,1)}, f32[4,3,8,512]{3,2,1,0:T(8,128)}, f32[16,7...) custom-call(bf16[2048,768]{1,0:T(8,128)(2,1)} %refs_0_.1, ...), custom_call_target="tpu_custom_call" | custom-call | tf_op jit(solution)/shard_map/front/pallas_call | solution.py:887
  92.0 96.3 %middle.1 = (bf16[2048,768]{1,0:T(8,128)(2,1)}, f32[2048,768]{1,0:T(8,128)}, bf16[2048,768]{1,0:T(8,128)(2,1)}, f32[16,768]{1,0:T(8,128)}, bf16[768,768]{1,0:T(8...) custom-call(bf16[2048,768]{1,0:T(8,128)(2,1)} %get-tuple-element.34.mixed_ref.refs_4_, ...), custom_call_target="tpu_custom_call" | custom-call | tf_op jit(solution)/shard_map/middle/pallas_call | solution.py:242
  188.3 101.4 %back.1 = (bf16[2048,768]{1,0:T(8,128)(2,1)}, f32[48,2304]{1,0:T(8,128)}, f32[48,768]{1,0:T(8,128)}, f32[48,3072]{1,0:T(8,128)}, f32[192,768]{1,0:T(8,128)}, /*index=5*/f32[16,768]{1,0:T(8,128)}) custom-call(bf16[2048,2304]{1,0:T(8,128)(2,1)} %get-tuple-element.41.refs_0_.refs_1_.refs_2_, bf16[2048,2304]{1,0:T(8,128)(2,1)} %get-tuple-element.41.refs_0_.refs_1_.refs_2_, ...), custom_call_target="tpu_custom_call" | custom-call | tf_op jit(solution)/shard_map/back/pallas_call | solution.py:1059
  289.7 0.7 slice.34
  290.4 0.7 slice.30
  291.2 0.1 constant_dynamic-slice_fusion
  291.2 0.6 dynamic_slice.7
  291.9 0.5 slice_bitcast_fusion
  292.4 0.6 fusion
  293.0 5.2 %convert_element_type.3 = f32[2048,768]{1,0:T(8,128)} convert(bf16[2048,768]{1,0:T(8,128)(2,1)} %get-tuple-element.50) | non-fusion elementwise | flops 1572864 | bytes 9437184 | tf_op jit(solution)/shard_map/convert_element_type | solution.py:1130
  298.2 0.0 copy-done.2
  298.2 0.8 copy.35
  299.0 0.0 copy-done.3
  299.0 0.7 copy.36
  299.6 0.0 copy-done.1
  299.6 0.8 copy.37
  300.4 0.8 copy.38
  (10 shorter events, 0.0 us)
Async XLA Ops:
  293.0 5.2 %copy-start.2 = (f32[48,2304]{1,0:T(8,128)S(1)}, f32[48,2304]{1,0:T(8,128)}, u32[]{:S(2)}) copy-start(f32[48,2304]{1,0:T(8,128)} %get-tuple-element.75) | copy-start | bytes 1327108
  293.0 6.0 %copy-start.3 = (f32[48,768]{1,0:T(8,128)S(1)}, f32[48,768]{1,0:T(8,128)}, u32[]{:S(2)}) copy-start(f32[48,768]{1,0:T(8,128)} %get-tuple-element.77) | copy-start | bytes 442372
  293.0 6.6 %copy-start.1 = (f32[48,3072]{1,0:T(8,128)S(1)}, f32[48,3072]{1,0:T(8,128)}, u32[]{:S(2)}) copy-start(f32[48,3072]{1,0:T(8,128)} %get-tuple-element.80) | copy-start | bytes 1769476
  293.0 7.5 %copy-start = (f32[192,768]{1,0:T(8,128)S(1)}, f32[192,768]{1,0:T(8,128)}, u32[]{:S(2)}) copy-start(f32[192,768]{1,0:T(8,128)} %get-tuple-element.82) | copy-start | bytes 1769476
